TPU v7x, 256 devices: a whole 4x4x8 slice. The times are simulated.
256 devices in a mesh: section: 64 (over z_hi, y, x, core), tp: 4 (over z_lo).
Axes of the slice: x: 4, y: 4, z: 8 (z_hi: 2, z_lo: 4; z = z_hi * 4 + z_lo), core: 2. Of those that a mesh axis runs over, the one named last changes fastest.
Arguments:
- param: float32 [4096, 3584], P('section', 'tp'), may hold values from -4 to 4
- moment_one: float32 [4096, 3584], P('section', 'tp'), may hold values from -2 to 2
- moment_two: float32 [4096, 3584], P('section', 'tp'), may hold values from 0.001 to 1
- proj_grad: float32 [4096, 3584], P('section', 'tp'), may hold values from -6 to 6
- embed_grad: bfloat16 [32768, 3584], P('section', 'tp'), may hold values from -6 to 6
- token_ids: int32 [32768], P('section'), may hold values from 0 to 4095, as said below
- next_ids: int32 [32768], P('section'), may hold values from 0 to 4095, as said below
Outputs:
- new_param: float32 [4096, 3584], P('section', 'tp')
- new_moment_one: float32 [4096, 3584], P('section', 'tp')
- new_moment_two: float32 [4096, 3584], P('section', 'tp')
- next_rows: bfloat16 [32768, 3584], P('section')
Inputs may be any that keep to these rules, and one draw needn't show every extreme that they name: `token_ids`: in each section index's block of 512 tokens at most 16 ids fall into any one owner's run of 64 table rows (id // 64); in every draw some owner receives exactly 16 from every block. `next_ids`: the same bound of 16 a block and an owner holds, and is reached, as for token_ids.
All inputs are finite; a program needn't handle non-finite values.
Results may differ from a plain program's by a relative error of at most 0.001.
Values may be sent and summed in bfloat16 or wider, within the bound.
No kernel may reach another device: no remote copies, remote signals or barrier semaphores. Data moves between devices by JAX's collectives and lax.ppermute only.
A program may use at most 64 MiB of HBM per device.

v0:
```python
import jax
import jax.numpy as jnp
from jax import lax
from jax.sharding import PartitionSpec as P

STEP = 1000


def slot_layout(ids, owners, cap, rows_own):
    owner = ids // rows_own
    hits = (owner[:, None] == jnp.arange(owners)[None, :]).astype(jnp.int32)
    before = jnp.cumsum(hits, axis=0) - hits
    rank = jnp.sum(before * hits, axis=1)
    return (owner * cap + rank, ids - owner * rows_own)


def on_device(param, moment_one, moment_two, proj_grad, embed_grad, token_ids, next_ids):
    rows_own, width = param.shape
    owners = lax.axis_size("section")
    tokens_here = token_ids.shape[0]
    cap = 2 * tokens_here // owners
    slot, local = slot_layout(token_ids, owners, cap, rows_own)
    outgoing = jnp.zeros((owners * cap, width), jnp.bfloat16).at[slot].set(embed_grad)
    targets = jnp.full((owners * cap,), -1, jnp.int32).at[slot].set(local)
    got_rows, got_local = (
        lax.all_to_all(
            outgoing.reshape(owners, cap, width), "section", split_axis=0, concat_axis=0, tiled=True
        ),
        lax.all_to_all(
            targets.reshape(owners, cap), "section", split_axis=0, concat_axis=0, tiled=True
        ),
    )
    select = (jnp.arange(rows_own)[:, None] == got_local.reshape(-1)[None, :]).astype(jnp.bfloat16)
    embed_sum = jnp.dot(
        select, got_rows.reshape(owners * cap, width), preferred_element_type=jnp.float32
    )
    grad = proj_grad + embed_sum
    new_moment_one = 0.9 * moment_one + 0.1 * grad
    new_moment_two = 0.999 * moment_two + 0.001 * grad * grad
    first_fix = 1.0 - 0.9**STEP
    second_fix = 1.0 - 0.999**STEP
    new_param = param - 0.01 * (new_moment_one / first_fix) / (
        jnp.sqrt(new_moment_two / second_fix) + 1e-08
    )
    table = new_param.astype(jnp.bfloat16)
    slot, local = slot_layout(next_ids, owners, cap, rows_own)
    asking = jnp.full((owners * cap,), -1, jnp.int32).at[slot].set(local).reshape(owners, cap)
    found = jnp.take(
        table,
        jnp.clip(
            lax.all_to_all(asking, "section", split_axis=0, concat_axis=0, tiled=True),
            0,
            rows_own - 1,
        ),
        axis=0,
    )
    replies = lax.all_to_all(found, "section", split_axis=0, concat_axis=0, tiled=True)
    mine = jnp.take(replies.reshape(owners * cap, width), slot, axis=0)
    next_rows = lax.all_gather(mine, "tp", axis=1, tiled=True)
    return (new_param, new_moment_one, new_moment_two, next_rows)


def solution(mesh):
    placed = (
        P("section", "tp"),
        P("section", "tp"),
        P("section", "tp"),
        P("section", "tp"),
        P("section", "tp"),
        P("section"),
        P("section"),
    )
    return jax.shard_map(
        on_device,
        mesh=mesh,
        in_specs=placed,
        out_specs=(P("section", "tp"), P("section", "tp"), P("section", "tp"), P("section", None)),
        check_vma=False,
    )
```

profile of v0, /device:TPU:230, one launch (start us, length us, event | category | flops | bytes accessed | tf_op | source)
XLA Modules:
  0.0 254.8 jit_solution(6298130976324283758)
XLA Ops:
  7.2 0.7 multiply_subtract_fusion
  7.9 1.2 reduce-window.16
  9.1 0.2 slice_reduce_fusion
  9.4 0.1 fusion.5
  9.5 2.4 scatter_custom_fusion.2
  11.9 0.7 all_to_all.21
  12.6 12.9 %all-to-all-start.2 = ((s32[64,1,16]{2,1,0:T(1,128)}), s32[64,1,16]{2,1,0:T(1,128)S(1)}, u32[]{:S(2)}, u32[]{:S(2)}) async-start(s32[64,1,16]{2,1,0:T(1,128)} %bitcast.7), calls=%async_computation.2 | async-start | bytes 65536 | tf_op jit(solution)/shard_map/all_to_all | solution.py:51
  25.6 0.7 multiply_subtract_fusion.1
  26.3 1.2 reduce-window.14
  27.5 0.2 slice_reduce_fusion.1
  27.7 0.1 fusion.8
  27.9 2.4 scatter_custom_fusion
  30.3 0.7 all_to_all.18
  31.0 12.8 %all-to-all-start = ((s32[64,1,16]{2,1,0:T(1,128)}), s32[64,1,16]{2,1,0:T(1,128)S(1)}, u32[]{:S(2)}, u32[]{:S(2)}) async-start(s32[64,1,16]{2,1,0:T(1,128)} %bitcast.2), calls=%async_computation | async-start | bytes 65536 | tf_op jit(solution)/shard_map/all_to_all | solution.py:29
  43.9 4.6 %scatter_custom_fusion.1 = bf16[1024,896]{1,0:T(8,128)(2,1)} fusion(s32[512]{0:T(512)S(1)} %compare_select_fusion.3, bf16[512,896]{1,0:T(8,128)(2,1)} %param.11, bf16[]{:T(256)} %constant.74.clone.1), kind=kCustom, calls=%fused_computation.7 | custom fusion | bytes 1835520 | tf_op jit(solution)/shard_map/scatter | solution.py:23
  48.4 0.8 all-to-all-done
  49.3 12.1 %all-to-all-start.1 = ((bf16[64,16,896]{2,1,0:T(8,128)(2,1)}), bf16[64,16,896]{2,1,0:T(8,128)(2,1)S(1)}, u32[]{:S(2)}, u32[]{:S(2)}) async-start(bf16[64,16,896]{2,1,0:T(8,128)(2,1)} %bitcast.56), calls=%async_computation.1 | async-start | bytes 3670016 | tf_op jit(solution)/shard_map/all_to_all | solution.py:26
  61.5 0.1 reshape.102
  61.6 0.5 broadcast.142
  62.1 0.7 reduce.7
  62.8 0.1 eq.69
  62.9 26.4 %all-to-all-done.1 = bf16[64,16,896]{2,1,0:T(8,128)(2,1)S(1)} async-done(((bf16[64,16,896]{2,1,0:T(8,128)(2,1)}), bf16[64,16,896]{2,1,0:T(8,128)(2,1)S(1)}, u32[]{:S(2)}, u32[]{:S(2)}) %all-to-all-start.1) | async-done | bytes 1835040 | tf_op jit(solution)/shard_map/all_to_all | solution.py:26
  89.3 1.3 fusion.20
  90.7 4.0 %gather_fusion = bf16[1024,896]{1,0:T(8,128)(2,1)S(1)} fusion(bf16[64,896]{1,0:T(8,128)(2,1)S(1)} %get-tuple-element.8, s32[1024]{0:T(1024)S(1)} %broadcast_clamp_fusion.1), kind=kCustom, calls=%fused_computation | custom fusion | bytes 3674112 | tf_op jit(solution)/shard_map/jit(_take)/gather | solution.py:48
  94.7 1.5 broadcast_select_fusion
  96.2 24.8 %all-to-all-start.3 = ((bf16[64,16,896]{2,1,0:T(8,128)(2,1)}), bf16[64,16,896]{2,1,0:T(8,128)(2,1)S(1)}, u32[]{:S(2)}, u32[]{:S(2)}) async-start(bf16[64,16,896]{2,1,0:T(8,128)(2,1)} %broadcast_select_fusion), calls=%async_computation.3 | async-start | bytes 3670016 | tf_op jit(solution)/shard_map/all_to_all | solution.py:57
  121.1 0.0 all-gather.2.cloned.1.call-start
  121.2 24.4 %all-to-all-done.3 = bf16[64,16,896]{2,1,0:T(8,128)(2,1)S(1)} async-done(((bf16[64,16,896]{2,1,0:T(8,128)(2,1)}), bf16[64,16,896]{2,1,0:T(8,128)(2,1)S(1)}, u32[]{:S(2)}, u32[]{:S(2)}) %all-to-all-start.3) | async-done | bytes 1835040 | tf_op jit(solution)/shard_map/all_to_all | solution.py:57
  145.6 2.0 gather_fusion.1
  147.7 1.1 broadcast_select_fusion.1
  148.8 95.1 %all-gather.2.cloned.1.call-done = bf16[512,3584]{1,0:T(8,128)(2,1)} async-done(((bf16[512,896]{1,0:T(8,128)(2,1)}), bf16[512,3584]{1,0:T(8,128)(2,1)}) %all-gather.2.cloned.1.call-update) | async-done | bytes 3670032 | tf_op jit(solution)/shard_map/all_gather | solution.py:59
  243.9 4.1 %copy.22 = bf16[512,3584]{1,0:T(8,128)(2,1)} copy(bf16[512,3584]{1,0:T(8,128)(2,1)} %all-gather.2.cloned.1.call-done) | data formatting | bytes 7340032
  (23 shorter events, 0.2 us)
Async XLA Ops:
  12.6 18.4 %all-to-all-start.2 = ((s32[64,1,16]{2,1,0:T(1,128)}), s32[64,1,16]{2,1,0:T(1,128)S(1)}, u32[]{:S(2)}, u32[]{:S(2)}) async-start(s32[64,1,16]{2,1,0:T(1,128)} %bitcast.7), calls=%async_computation.2 | async-start | bytes 65536 | tf_op jit(solution)/shard_map/all_to_all | solution.py:51
  31.0 18.2 %all-to-all-start = ((s32[64,1,16]{2,1,0:T(1,128)}), s32[64,1,16]{2,1,0:T(1,128)S(1)}, u32[]{:S(2)}, u32[]{:S(2)}) async-start(s32[64,1,16]{2,1,0:T(1,128)} %bitcast.2), calls=%async_computation | async-start | bytes 65536 | tf_op jit(solution)/shard_map/all_to_all | solution.py:29
  49.3 40.0 %copy-start = (f32[64,896]{1,0:T(8,128)S(1)}, f32[64,896]{1,0:T(8,128)}, u32[]{:S(2)}) copy-start(f32[64,896]{1,0:T(8,128)} %param.7) | copy-start | bytes 688132
  49.3 40.0 %copy-start.1 = (f32[64,896]{1,0:T(8,128)S(1)}, f32[64,896]{1,0:T(8,128)}, u32[]{:S(2)}) copy-start(f32[64,896]{1,0:T(8,128)} %param.8) | copy-start | bytes 688132
  49.3 40.0 %copy-start.2 = (f32[64,896]{1,0:T(8,128)S(1)}, f32[64,896]{1,0:T(8,128)}, u32[]{:S(2)}) copy-start(f32[64,896]{1,0:T(8,128)} %param.9) | copy-start | bytes 688132
  49.3 40.0 %copy-start.3 = (f32[64,896]{1,0:T(8,128)S(1)}, f32[64,896]{1,0:T(8,128)}, u32[]{:S(2)}) copy-start(f32[64,896]{1,0:T(8,128)} %param.10) | copy-start | bytes 688132
  49.3 40.0 %all-to-all-start.1 = ((bf16[64,16,896]{2,1,0:T(8,128)(2,1)}), bf16[64,16,896]{2,1,0:T(8,128)(2,1)S(1)}, u32[]{:S(2)}, u32[]{:S(2)}) async-start(bf16[64,16,896]{2,1,0:T(8,128)(2,1)} %bitcast.56), calls=%async_computation.1 | async-start | bytes 3670016 | tf_op jit(solution)/shard_map/all_to_all | solution.py:26
  96.2 49.3 %all-to-all-start.3 = ((bf16[64,16,896]{2,1,0:T(8,128)(2,1)}), bf16[64,16,896]{2,1,0:T(8,128)(2,1)S(1)}, u32[]{:S(2)}, u32[]{:S(2)}) async-start(bf16[64,16,896]{2,1,0:T(8,128)(2,1)} %broadcast_select_fusion), calls=%async_computation.3 | async-start | bytes 3670016 | tf_op jit(solution)/shard_map/all_to_all | solution.py:57
  121.1 122.8 %all-gather.2.cloned.1.call-start = ((), (), s32[]{:S(2)}) async-start(), calls=%async_computation.4 | async-start | bytes 4587520 | tf_op jit(solution)/shard_map/all_gather | solution.py:59
Sparse Core Ops, SparseCore 0:
  148.9 94.9 all-gather.1
where the time goes:
time: 257 us; the launch traced here: 255 us
  waiting for transfers between devices  147 us (57%)
  starting transfers between devices  62.7 us (24%)
  local copies, waits for them, and re-layouts  22.2 us (9%)
  between operations  14.2 us (6%)
  other arithmetic  7.61 us (3%)
    all_gather x1, waiting for transfers between devices, on_device(): next_rows = lax.all_gather(mine, 'tp', axis=1, tiled=True)  95.1 us
    all_to_all x1, waiting for transfers between devices, on_device(): lax.all_to_all(outgoing.reshape(owners, cap, width), 'section', split_axi...  26.4 us
    all_to_all x1, starting transfers between devices, on_device(): lax.all_to_all(found, 'section', split_axis=0, concat_axis=0, tiled=True)  24.8 us
    all_to_all x1, waiting for transfers between devices, on_device(): lax.all_to_all(found, 'section', split_axis=0, concat_axis=0, tiled=True)  24.4 us
    all_to_all x1, starting transfers between devices, on_device(): lax.all_to_all(asking, 'section', split_axis=0, concat_axis=0, tiled=True)  12.9 us
    all_to_all x1, starting transfers between devices, on_device(): lax.all_to_all(targets.reshape(owners, cap), 'section', split_axis=0, con...  12.8 us
    all_to_all x1, starting transfers between devices, on_device(): lax.all_to_all(outgoing.reshape(owners, cap, width), 'section', split_axi...  12.1 us
  transfers between devices with their start and end apart: 5, of which 4 were waited for; matrix products, arithmetic and copies ran while one was open for 4% of the time, Pallas kernels for 0%

commit v1 on v0

v1 whole, which is shorter than its diff:
```python
import functools

import jax
import jax.numpy as jnp
from jax import lax
from jax.experimental import pallas as pl
from jax.experimental.pallas import tpu as pltpu
from jax.sharding import Mesh, PartitionSpec as P

STEP = 1000
PLANE = ("y", "x", "c")
SECTION = ("zh",) + PLANE
PAIR = [(0, 1), (1, 0)]
LANES = 128
VMEM = pl.BlockSpec(memory_space=pltpu.VMEM)
SMEM = pl.BlockSpec(memory_space=pltpu.SMEM)
ANY = pl.BlockSpec(memory_space=pl.ANY)
BF16, F32, I32 = jnp.bfloat16, jnp.float32, jnp.int32


def iota(shape, dim):
    return lax.broadcasted_iota(I32, shape, dim)


def call(body, out, n_in, specs=None, out_specs=None, cost=(0, 0), scratch=(), name=None, vmem=20):
    return pl.pallas_call(
        body,
        out_shape=out,
        in_specs=specs or [VMEM] * n_in,
        out_specs=out_specs or jax.tree.map(lambda _: VMEM, out),
        scratch_shapes=scratch,
        name=name,
        compiler_params=pltpu.CompilerParams(vmem_limit_bytes=vmem << 20),
        cost_estimate=pl.CostEstimate(flops=cost[0], bytes_accessed=cost[1], transcendentals=0),
    )


def split_ids(ids, rows_own, places):
    owner = ids // rows_own
    return owner % places, ids + (owner // places - owner) * rows_own


def slots_of_row(ids, rows_own, places, per_place):
    tokens = ids.shape[1]
    place, local = split_ids(ids, rows_own, places)
    hits = iota((places, tokens), 0) == place
    earlier = (iota((tokens, tokens), 0) < iota((tokens, tokens), 1)).astype(BF16)
    before = jnp.dot(hits.astype(BF16), earlier, preferred_element_type=F32)
    rank = jnp.sum(jnp.where(hits, before, 0.0), axis=0, keepdims=True).astype(I32)
    return place * per_place + rank, local


def pack_body(places, rows_own, token_ref, next_ref, grad_ref, out_ref):
    tokens, width = grad_ref.shape
    slots = out_ref.shape[0]
    per_place = slots // places
    tags = jnp.zeros((slots, LANES), F32)
    for lane, ids_ref in enumerate((token_ref, next_ref)):
        slot, local = slots_of_row(ids_ref[...], rows_own, places, per_place)
        chosen = (iota((slots, tokens), 0) == slot).astype(BF16)
        if lane == 0:
            out_ref[:, :width] = jnp.dot(chosen, grad_ref[...], preferred_element_type=F32).astype(BF16)
        marks = jnp.where(iota((LANES, tokens), 0) == lane, local + 1, 0).astype(F32).astype(BF16)
        tags += lax.dot_general(chosen, marks, (((1,), (1,)), ((), ())), preferred_element_type=F32)
    out_ref[:, width:] = tags.astype(BF16)


def chosen_rows(got_ref, lane, width, rows, half_ref):
    tag = got_ref[:, width + lane : width + lane + 1].astype(F32).astype(I32) - 1
    row = iota((got_ref.shape[0], rows), 1)
    half = rows // 2
    mine_first = jnp.where(row < half, row + half_ref[0] * half, row - half_ref[0] * half)
    return (tag == mine_first).astype(F32).astype(BF16)


def sum_body(half_ref, got_ref, mine_ref, other_ref):
    half, width = mine_ref.shape
    chosen = chosen_rows(got_ref, 0, width, 2 * half, half_ref)
    total = lax.dot_general(
        chosen, got_ref[:, :width], (((0,), (0,)), ((), ())), preferred_element_type=F32
    )
    mine_ref[...] = total[:half]
    other_ref[...] = total[half:]


def ask_body(half_ref, got_ref, out_ref):
    out_ref[...] = chosen_rows(got_ref, 1, got_ref.shape[1] - LANES, out_ref.shape[1], half_ref)


def adam_body(param_ref, one_ref, two_ref, proj_ref, mine_ref, other_ref, p_ref, o_ref, t_ref, table_ref):
    grad = proj_ref[...] + (mine_ref[...] + other_ref[...])
    one = 0.9 * one_ref[...] + 0.1 * grad
    two = 0.999 * two_ref[...] + 0.001 * grad * grad
    first_fix = 1.0 - 0.9**STEP
    second_fix = 1.0 - 0.999**STEP
    param = param_ref[...] - 0.01 * (one / first_fix) / (jnp.sqrt(two / second_fix) + 1e-08)
    o_ref[...] = one
    t_ref[...] = two
    p_ref[...] = param
    table_ref[...] = param.astype(BF16)


def find_body(chosen_ref, mine_ref, other_ref, out_ref):
    half = mine_ref.shape[0]
    found = jnp.dot(chosen_ref[:, :half], mine_ref[...], preferred_element_type=F32)
    found += jnp.dot(chosen_ref[:, half:], other_ref[...], preferred_element_type=F32)
    out_ref[...] = found.astype(BF16)


def route_body(places, rows_own, ids_ref, out_ref):
    tokens, slots = out_ref.shape
    place, _ = split_ids(ids_ref[...], rows_own, places)
    hits = iota((tokens, LANES), 1) == place
    earlier = (iota((tokens, tokens), 1) < iota((tokens, tokens), 0)).astype(BF16)
    before = jnp.dot(earlier, hits.astype(BF16), preferred_element_type=F32)
    rank = jnp.sum(jnp.where(hits, before, 0.0), axis=1, keepdims=True).astype(I32)
    slot = place * (slots // places) + rank
    out_ref[...] = (iota((tokens, slots), 1) == slot).astype(BF16)


def pick_body(route_ref, replies_ref, out_ref):
    out_ref[...] = jnp.dot(route_ref[...], replies_ref[...], preferred_element_type=F32).astype(BF16)


def join_body(ranks, me_ref, own_ref, *refs):
    ups, downs = refs[: ranks - 1], refs[ranks - 1 : 2 * ranks - 2]
    out_ref, sems = refs[-2:]
    me = me_ref[0]
    width = own_ref.shape[1]

    def copy(src, rank, sem):
        columns = pl.ds(pl.multiple_of(rank * width, LANES), width)
        return pltpu.make_async_copy(src, out_ref.at[:, columns], sems.at[sem])

    copies = [(None, copy(own_ref, me, 0))]
    for k in range(1, ranks):
        copies.append((me >= k, copy(ups[k - 1], jnp.maximum(me - k, 0), k)))
        copies.append((me + k < ranks, copy(downs[k - 1], jnp.minimum(me + k, ranks - 1), ranks - 1 + k)))
    for cond, c in copies:
        if cond is None:
            c.start()
        else:
            pl.when(cond)(c.start)
    for cond, c in copies:
        if cond is None:
            c.wait()
        else:
            pl.when(cond)(c.wait)


def on_device(param, moment_one, moment_two, proj_grad, embed_grad, token_ids, next_ids):
    rows_own, width = param.shape
    places = lax.axis_size(PLANE)
    ranks = lax.axis_size("tp")
    tokens = token_ids.shape[0]
    slots = 2 * tokens
    sds = jax.ShapeDtypeStruct
    half = lax.axis_index("zh").reshape(1)
    me = lax.axis_index("tp").reshape(1)

    packed = call(
        functools.partial(pack_body, places, rows_own), sds((slots, width + LANES), BF16), 3,
        cost=(2 * slots * tokens * width, 4 << 20), name="pack",
    )(token_ids.reshape(1, -1), next_ids.reshape(1, -1), embed_grad)
    got = lax.all_to_all(
        packed.reshape(places, slots // places, width + LANES), PLANE, split_axis=0, concat_axis=0, tiled=True
    ).reshape(slots, width + LANES)
    route = call(
        functools.partial(route_body, places, rows_own), sds((tokens, slots), BF16), 1,
        cost=(2 * tokens * tokens * LANES, 2 << 20), name="route",
    )(next_ids.reshape(-1, 1))
    mine, other = call(
        sum_body, (sds((rows_own, width), F32),) * 2, 2, specs=[SMEM, VMEM],
        cost=(4 * slots * rows_own * width, 3 << 20), name="sum",
    )(half, got)
    theirs = lax.ppermute(other, "zh", PAIR)
    chosen = call(
        ask_body, sds((slots, 2 * rows_own), BF16), 2, specs=[SMEM, VMEM],
        cost=(slots * LANES, 1 << 20), name="ask",
    )(half, got)
    block = sds((rows_own, width), F32)
    new_param, new_one, new_two, table = call(
        adam_body, (block, block, block, sds((rows_own, width), BF16)), 6,
        cost=(20 * rows_own * width, 2 << 20), name="adam",
    )(param, moment_one, moment_two, proj_grad, mine, theirs)
    table_other = lax.ppermute(table, "zh", PAIR)
    found = call(
        find_body, sds((slots, width), BF16), 3, cost=(4 * slots * rows_own * width, 3 << 20), name="find",
    )(chosen, table, table_other)
    replies = lax.all_to_all(
        found.reshape(places, slots // places, width), PLANE, split_axis=0, concat_axis=0, tiled=True
    ).reshape(slots, width)
    own = call(
        pick_body, sds((tokens, width), BF16), 2, cost=(2 * slots * tokens * width, 4 << 20), name="pick",
    )(route, replies)
    ups, downs = [], []
    up = down = own
    for k in range(1, ranks):
        up = lax.ppermute(up, "tp", [(i, i + 1) for i in range(k - 1, ranks - 1)])
        down = lax.ppermute(down, "tp", [(i, i - 1) for i in range(1, ranks - k + 1)])
        ups.append(up)
        downs.append(down)
    next_rows = call(
        functools.partial(join_body, ranks), sds((tokens, ranks * width), BF16), 0,
        specs=[SMEM] + [ANY] * (2 * ranks - 1), out_specs=ANY,
        scratch=[pltpu.SemaphoreType.DMA((2 * ranks - 1,))],
        cost=(0, 8 << 20), name="join",
    )(me, own, *ups, *downs)
    return (new_param, new_one, new_two, next_rows)


def solution(mesh):
    grid = Mesh(mesh.devices.reshape(2, 4, 4, 2, mesh.shape["tp"]), SECTION + ("tp",))
    block = P(SECTION, "tp")
    return jax.shard_map(
        on_device,
        mesh=grid,
        in_specs=(block,) * 5 + (P(SECTION),) * 2,
        out_specs=(block,) * 3 + (P(SECTION, None),),
        check_vma=False,
    )
```

time: 257 us -> 239 us (0.930)
  Pallas kernels: 0 us -> 66.1 us
  starting transfers between devices: 62.7 us -> 27.7 us
  local copies, waits for them, and re-layouts: 22.2 us -> 6.12 us
  between operations: 14.2 us -> 0.84 us
  waiting for transfers between devices: 147 us -> 137 us
  other arithmetic: 7.61 us -> 0 us
    all_gather x1 -> x0, waiting for transfers between devices: 95.1 us -> none  [on_device(): next_rows = lax.all_gather(mine, 'tp', axis=1, tiled=True)]
    ppermute x0 -> x8, waiting for transfers between devices: none -> 90.4 us  [the longest x3 49.3 us: on_device(): up = lax.ppermute(up, 'tp', [(i, i + 1) for i in range(k - 1, ranks - 1)])]
    pallas_call x0 -> x8, Pallas kernels: none -> 66.1 us  [the longest x1 56.7 us: on_device(): call(functools.partial(join_body, ranks), sds((tokens, ranks * width), BF...]
    all_to_all x4 -> x2, starting transfers between devices: 62.7 us -> 15.9 us  [the longest x1 8.32 us: on_device(): lax.all_to_all(found.reshape(places, slots // places, width), PLANE, spli...]
    ppermute x0 -> x8, starting transfers between devices: none -> 11.9 us  [the longest x3 6.48 us: on_device(): lax.ppermute(down, 'tp', [(i, i - 1) for i in range(1, ranks - k + 1)])]
    scatter x3 -> x0, local copies, waits for them, and re-layouts: 9.47 us -> none  [the longest x1 4.58 us: on_device(): jnp.zeros((owners * cap, width), jnp.bfloat16).at[slot].set(embed_grad)]
    gather x2 -> x0, local copies, waits for them, and re-layouts: 6.09 us -> none  [the longest x1 4.04 us: on_device(): jnp.take(table, jnp.clip(lax.all_to_all(asking, 'section', split_axis=0,...]
    all_to_all x4 -> x2, waiting for transfers between devices: 51.7 us -> 46.8 us  [the longest x1 25.4 us: on_device(): lax.all_to_all(packed.reshape(places, slots // places, width + LANES), PL...]
  transfers between devices with their start and end apart: 5 -> 10, of which waited for: 4 -> 8; matrix products, arithmetic and copies ran while one was open for 4% -> 0% of each run, Pallas kernels for 0% -> 1%
where the time goes in v1:
time: 239 us; the launch traced here: 238 us
  waiting for transfers between devices  137 us (57%)
  Pallas kernels  66.1 us (28%)
  starting transfers between devices  27.7 us (12%)
  local copies, waits for them, and re-layouts  6.12 us (3%)
    pallas_call x1, Pallas kernels, on_device(): call(functools.partial(join_body, ranks), sds((tokens, ranks * width), BF...  56.7 us
    ppermute x3, waiting for transfers between devices, on_device(): up = lax.ppermute(up, 'tp', [(i, i + 1) for i in range(k - 1, ranks - 1)])  49.3 us
    all_to_all x1, waiting for transfers between devices, on_device(): lax.all_to_all(packed.reshape(places, slots // places, width + LANES), PL...  25.4 us
    all_to_all x1, waiting for transfers between devices, on_device(): lax.all_to_all(found.reshape(places, slots // places, width), PLANE, spli...  21.5 us
    ppermute x3, waiting for transfers between devices, on_device(): lax.ppermute(down, 'tp', [(i, i - 1) for i in range(1, ranks - k + 1)])  17.2 us
    ppermute x1, waiting for transfers between devices, on_device(): theirs = lax.ppermute(other, 'zh', PAIR)  13.7 us
    ppermute x1, waiting for transfers between devices, on_device(): table_other = lax.ppermute(table, 'zh', PAIR)  10.2 us
    all_to_all x1, starting transfers between devices, on_device(): lax.all_to_all(found.reshape(places, slots // places, width), PLANE, spli...  8.32 us
  transfers between devices with their start and end apart: 10, of which 8 were waited for; matrix products, arithmetic and copies ran while one was open for 0% of the time, Pallas kernels for 1%

profile of v1, /device:TPU:230, one launch (start us, length us, event | category | flops | bytes accessed | tf_op | source)
XLA Modules:
  0.0 238.0 jit_solution(5455356846204445565)
XLA Ops:
  0.6 0.7 copy-done.7
  1.3 1.2 copy-done.9
  2.5 0.7 copy-done.10
  3.2 2.7 %pack.1 = bf16[1024,1024]{1,0:T(8,128)(2,1)S(1)} custom-call(s32[1,512]{1,0:T(1,128)S(1)} %bitcast.15, s32[1,512]{1,0:T(1,128)S(1)} %bitcast.13, bf16[512,896]{1,0:T(8,128)(2,1)S(1)} %copy-done.9), custom_call_target="tpu_custom_call" | custom-call | flops 939524096 | bytes 4194304 | tf_op jit(solution)/shard_map/pack/pallas_call | solution.py:161
  5.9 1.3 copy-done.2
  7.2 7.6 %all-to-all-start = ((bf16[32,32,1024]{2,1,0:T(8,128)(2,1)}), bf16[32,32,1024]{2,1,0:T(8,128)(2,1)S(1)}, u32[]{:S(2)}, u32[]{:S(2)}) async-start(bf16[32,32,1024]{2,1,0:T(8,128)(2,1)} %bitcast.12), calls=%async_computation | async-start | bytes 4194304 | tf_op jit(solution)/shard_map/all_to_all | solution.py:165
  14.9 25.4 %all-to-all-done = bf16[32,32,1024]{2,1,0:T(8,128)(2,1)S(1)} async-done(((bf16[32,32,1024]{2,1,0:T(8,128)(2,1)}), bf16[32,32,1024]{2,1,0:T(8,128)(2,1)S(1)}, u32[]{:S(2)}, u32[]{:S(2)}) %all-to-all-start) | async-done | bytes 2097184 | tf_op jit(solution)/shard_map/all_to_all | solution.py:165
  40.2 0.7 sum.1
  41.0 1.5 collective-permute-start
  42.5 13.7 %collective-permute-done.other_ref = f32[64,896]{1,0:T(8,128)S(1)} collective-permute-done((f32[64,896]{1,0:T(8,128)S(1)}, f32[64,896]{1,0:T(8,128)S(1)}, u32[]{:S(2)}, u32[]{:S(2)}) %collective-permute-start) | collective-permute-done | bytes 229408 | tf_op jit(solution)/shard_map/ppermute | solution.py:176
  56.2 1.0 adam.1
  57.2 0.2 ask.1.chosen_ref
  57.4 10.2 %collective-permute-done.1.other_ref = bf16[64,896]{1,0:T(8,128)(2,1)S(1)} collective-permute-done((bf16[64,896]{1,0:T(8,128)(2,1)S(1)}, bf16[64,896]{1,0:T(8,128)(2,1)S(1)}, u32[]{:S(2)}, u32[]{:S(2)}) %collective-permute-start.1) | collective-permute-done | bytes 114720 | tf_op jit(solution)/shard_map/ppermute | solution.py:186
  67.6 2.4 %find.1 = bf16[1024,896]{1,0:T(8,128)(2,1)} custom-call(bf16[1024,128]{1,0:T(8,128)(2,1)S(1)} %ask.1.chosen_ref, bf16[64,896]{1,0:T(8,128)(2,1)S(1)} %get-tuple-element.15.mine_ref, bf16[64,896]{1,0:T(8,128)(2,1)S(1)} %collective-permute-done.1.other_ref), custom_call_target="tpu_custom_call" | custom-call | flops 234881024 | bytes 3145728 | tf_op jit(solution)/shard_map/find/pallas_call | solution.py:187
  70.0 8.3 %all-to-all-start.1 = ((bf16[32,32,896]{2,1,0:T(8,128)(2,1)}), bf16[32,32,896]{2,1,0:T(8,128)(2,1)S(1)}, u32[]{:S(2)}, u32[]{:S(2)}) async-start(bf16[32,32,896]{2,1,0:T(8,128)(2,1)} %bitcast.7), calls=%async_computation.1 | async-start | bytes 3670016 | tf_op jit(solution)/shard_map/all_to_all | solution.py:190
  78.4 0.1 copy.11.ids_ref
  78.5 1.1 route.1.route_ref
  79.6 21.5 %all-to-all-done.1 = bf16[32,32,896]{2,1,0:T(8,128)(2,1)S(1)} async-done(((bf16[32,32,896]{2,1,0:T(8,128)(2,1)}), bf16[32,32,896]{2,1,0:T(8,128)(2,1)S(1)}, u32[]{:S(2)}, u32[]{:S(2)}) %all-to-all-start.1) | async-done | bytes 1835040 | tf_op jit(solution)/shard_map/all_to_all | solution.py:190
  101.1 1.2 pick.1.own_ref
  102.3 4.2 %collective-permute-start.5 = (bf16[512,896]{1,0:T(8,128)(2,1)S(1)}, bf16[512,896]{1,0:T(8,128)(2,1)S(1)}, u32[]{:S(2)}, u32[]{:S(2)}) collective-permute-start(bf16[512,896]{1,0:T(8,128)(2,1)S(1)} %pick.1.own_ref), channel_id=1, source_target_pairs={{1,0},{2,1},{3,2},{5,4},{6,5},{7,6},{9,8},{10,9},{11,10},{13,12},{... | collective-permute-start | bytes 2752520 | tf_op jit(solution)/shard_map/ppermute | solution.py:200
  106.5 1.3 collective-permute-start.2
  107.8 0.9 copy-done
  108.7 17.2 %collective-permute-done.5.refs_3_ = bf16[512,896]{1,0:T(8,128)(2,1)S(1)} collective-permute-done((bf16[512,896]{1,0:T(8,128)(2,1)S(1)}, bf16[512,896]{1,0:T(8,128)(2,1)S(1)}, u32[]{:S(2)}, u32[]{:S(2)}) %collective-permute-start.5) | collective-permute-done | bytes 917536 | tf_op jit(solution)/shard_map/ppermute | solution.py:200
  125.9 0.7 collective-permute-start.6
  126.6 4.0 %collective-permute-done.2.refs_0_ = bf16[512,896]{1,0:T(8,128)(2,1)S(1)} collective-permute-done((bf16[512,896]{1,0:T(8,128)(2,1)S(1)}, bf16[512,896]{1,0:T(8,128)(2,1)S(1)}, u32[]{:S(2)}, u32[]{:S(2)}) %collective-permute-start.2) | collective-permute-done | bytes 917536 | tf_op jit(solution)/shard_map/ppermute | solution.py:199
  130.6 1.3 collective-permute-start.3
  131.9 1.6 collective-permute-start.7
  133.5 22.2 %collective-permute-done.3.refs_1_ = bf16[512,896]{1,0:T(8,128)(2,1)} collective-permute-done((bf16[512,896]{1,0:T(8,128)(2,1)S(1)}, bf16[512,896]{1,0:T(8,128)(2,1)}, u32[]{:S(2)}, u32[]{:S(2)}) %collective-permute-start.3) | collective-permute-done | bytes 917536 | tf_op jit(solution)/shard_map/ppermute | solution.py:199
  155.7 1.3 collective-permute-start.4
  157.0 23.1 %collective-permute-done.4.refs_2_ = bf16[512,896]{1,0:T(8,128)(2,1)} collective-permute-done((bf16[512,896]{1,0:T(8,128)(2,1)}, bf16[512,896]{1,0:T(8,128)(2,1)}, u32[]{:S(2)}, u32[]{:S(2)}) %collective-permute-start.4) | collective-permute-done | bytes 917536 | tf_op jit(solution)/shard_map/ppermute | solution.py:199
  180.1 1.2 copy-done.1
  181.3 56.7 %join.1 = bf16[512,3584]{1,0:T(8,128)(2,1)} custom-call(s32[1]{0:T(128)} %bitcast.5.me_ref, bf16[512,896]{1,0:T(8,128)(2,1)S(1)} %copy-done.1, bf16[512,896]{1,0:T(8,128)(2,1)S(1)} %collective-permute-done.2.refs_0_, bf16[512,896]{1,0:T(8,128)(2,1)} %collective-permute-done.3.refs_1_, bf16[512,896]{1,0:T(8,128)(2,1)} %collective-permute-done.4.refs_2_, ...), custom_call_target="tpu_custom_call" | custom-call | bytes 8388608 | tf_op jit(solution)/shard_map/join/pallas_call | solution.py:203
  (19 shorter events, 0.1 us)
Async XLA Ops:
  0.6 0.7 copy-start.7
  1.3 1.2 copy-start.9
  2.5 0.7 copy-start.10
  5.9 1.3 copy-start.2
  7.2 33.0 %all-to-all-start = ((bf16[32,32,1024]{2,1,0:T(8,128)(2,1)}), bf16[32,32,1024]{2,1,0:T(8,128)(2,1)S(1)}, u32[]{:S(2)}, u32[]{:S(2)}) async-start(bf16[32,32,1024]{2,1,0:T(8,128)(2,1)} %bitcast.12), calls=%async_computation | async-start | bytes 4194304 | tf_op jit(solution)/shard_map/all_to_all | solution.py:165
  14.8 41.4 %copy-start.3 = (f32[64,896]{1,0:T(8,128)S(1)}, f32[64,896]{1,0:T(8,128)}, u32[]{:S(2)}) copy-start(f32[64,896]{1,0:T(8,128)} %param_ref.1) | copy-start | bytes 688132
  14.8 41.4 %copy-start.4 = (f32[64,896]{1,0:T(8,128)S(1)}, f32[64,896]{1,0:T(8,128)}, u32[]{:S(2)}) copy-start(f32[64,896]{1,0:T(8,128)} %one_ref.1) | copy-start | bytes 688132
  14.8 41.3 %copy-start.5 = (f32[64,896]{1,0:T(8,128)S(1)}, f32[64,896]{1,0:T(8,128)}, u32[]{:S(2)}) copy-start(f32[64,896]{1,0:T(8,128)} %two_ref.1) | copy-start | bytes 688132
  14.9 41.3 %copy-start.6 = (f32[64,896]{1,0:T(8,128)S(1)}, f32[64,896]{1,0:T(8,128)}, u32[]{:S(2)}) copy-start(f32[64,896]{1,0:T(8,128)} %proj_ref.1) | copy-start | bytes 688132
  41.0 15.2 %collective-permute-start = (f32[64,896]{1,0:T(8,128)S(1)}, f32[64,896]{1,0:T(8,128)S(1)}, u32[]{:S(2)}, u32[]{:S(2)}) collective-permute-start(f32[64,896]{1,0:T(8,128)S(1)} %get-tuple-element.11), channel_id=1, source_target_pairs={{0,128},{128,0},{1,129},{129,1},{2,130},{130,2},{3,131},{131,3},{4... | collective-permute-start | bytes 688136 | tf_op jit(solution)/shard_map/ppermute | solution.py:176
  57.2 10.5 %collective-permute-start.1 = (bf16[64,896]{1,0:T(8,128)(2,1)S(1)}, bf16[64,896]{1,0:T(8,128)(2,1)S(1)}, u32[]{:S(2)}, u32[]{:S(2)}) collective-permute-start(bf16[64,896]{1,0:T(8,128)(2,1)S(1)} %get-tuple-element.15.mine_ref), channel_id=1, source_target_pairs={{0,128},{128,0},{1,129},{129,1},{2,130},{130,2},{3,131},{131,3},{4... | collective-permute-start | bytes 344072 | tf_op jit(solution)/shard_map/ppermute | solution.py:186
  70.0 8.3 %copy-start.8 = (s32[512]{0:T(512)S(1)}, s32[512]{0:T(512)}, u32[]{:S(2)}) copy-start(s32[512]{0:T(512)} %param.13) | copy-start | bytes 6148
  70.0 31.0 %all-to-all-start.1 = ((bf16[32,32,896]{2,1,0:T(8,128)(2,1)}), bf16[32,32,896]{2,1,0:T(8,128)(2,1)S(1)}, u32[]{:S(2)}, u32[]{:S(2)}) async-start(bf16[32,32,896]{2,1,0:T(8,128)(2,1)} %bitcast.7), calls=%async_computation.1 | async-start | bytes 3670016 | tf_op jit(solution)/shard_map/all_to_all | solution.py:190
  102.3 23.5 %collective-permute-start.5 = (bf16[512,896]{1,0:T(8,128)(2,1)S(1)}, bf16[512,896]{1,0:T(8,128)(2,1)S(1)}, u32[]{:S(2)}, u32[]{:S(2)}) collective-permute-start(bf16[512,896]{1,0:T(8,128)(2,1)S(1)} %pick.1.own_ref), channel_id=1, source_target_pairs={{1,0},{2,1},{3,2},{5,4},{6,5},{7,6},{9,8},{10,9},{11,10},{13,12},{... | collective-permute-start | bytes 2752520 | tf_op jit(solution)/shard_map/ppermute | solution.py:200
  106.5 24.1 %collective-permute-start.2 = (bf16[512,896]{1,0:T(8,128)(2,1)S(1)}, bf16[512,896]{1,0:T(8,128)(2,1)S(1)}, u32[]{:S(2)}, u32[]{:S(2)}) collective-permute-start(bf16[512,896]{1,0:T(8,128)(2,1)S(1)} %pick.1.own_ref), channel_id=1, source_target_pairs={{0,1},{1,2},{2,3},{4,5},{5,6},{6,7},{8,9},{9,10},{10,11},{12,13},{... | collective-permute-start | bytes 2752520 | tf_op jit(solution)/shard_map/ppermute | solution.py:199
  107.8 0.9 copy-start
  125.9 6.0 %collective-permute-start.6 = (bf16[512,896]{1,0:T(8,128)(2,1)S(1)}, bf16[512,896]{1,0:T(8,128)(2,1)S(1)}, u32[]{:S(2)}, u32[]{:S(2)}) collective-permute-start(bf16[512,896]{1,0:T(8,128)(2,1)S(1)} %collective-permute-done.5.refs_3_), channel_id=1, source_target_pairs={{1,0},{2,1},{5,4},{6,5},{9,8},{10,9},{13,12},{14,13},{17,16},{18,1... | collective-permute-start | bytes 2752520 | tf_op jit(solution)/shard_map/ppermute | solution.py:200
  130.6 25.1 %collective-permute-start.3 = (bf16[512,896]{1,0:T(8,128)(2,1)S(1)}, bf16[512,896]{1,0:T(8,128)(2,1)}, u32[]{:S(2)}, u32[]{:S(2)}) collective-permute-start(bf16[512,896]{1,0:T(8,128)(2,1)S(1)} %collective-permute-done.2.refs_0_), channel_id=1, source_target_pairs={{1,2},{2,3},{5,6},{6,7},{9,10},{10,11},{13,14},{14,15},{17,18},{18... | collective-permute-start | bytes 2752520 | tf_op jit(solution)/shard_map/ppermute | solution.py:199
  131.9 25.1 %collective-permute-start.7 = (bf16[512,896]{1,0:T(8,128)(2,1)S(1)}, bf16[512,896]{1,0:T(8,128)(2,1)}, u32[]{:S(2)}, u32[]{:S(2)}) collective-permute-start(bf16[512,896]{1,0:T(8,128)(2,1)S(1)} %collective-permute-done.6.refs_4_), channel_id=1, source_target_pairs={{1,0},{5,4},{9,8},{13,12},{17,16},{21,20},{25,24},{29,28},{33,32},... | collective-permute-start | bytes 2752520 | tf_op jit(solution)/shard_map/ppermute | solution.py:200
  155.7 24.4 %collective-permute-start.4 = (bf16[512,896]{1,0:T(8,128)(2,1)}, bf16[512,896]{1,0:T(8,128)(2,1)}, u32[]{:S(2)}, u32[]{:S(2)}) collective-permute-start(bf16[512,896]{1,0:T(8,128)(2,1)} %collective-permute-done.3.refs_1_), channel_id=1, source_target_pairs={{2,3},{6,7},{10,11},{14,15},{18,19},{22,23},{26,27},{30,31},{34,35... | collective-permute-start | bytes 2752520 | tf_op jit(solution)/shard_map/ppermute | solution.py:199
  180.1 1.2 copy-start.1

commit v2 on v1

--- a/solution.py
+++ b/solution.py
@@ -50,19 +50,44 @@
     return place * per_place + rank, local
 
 
-def pack_body(places, rows_own, token_ref, next_ref, grad_ref, out_ref):
+def pack_body(places, rows_own, token_ref, next_ref, grad_ref, out_ref, slot_ref):
     tokens, width = grad_ref.shape
-    slots = out_ref.shape[0]
-    per_place = slots // places
-    tags = jnp.zeros((slots, LANES), F32)
-    for lane, ids_ref in enumerate((token_ref, next_ref)):
-        slot, local = slots_of_row(ids_ref[...], rows_own, places, per_place)
-        chosen = (iota((slots, tokens), 0) == slot).astype(BF16)
+    rows = out_ref.shape[0]
+    step = pl.program_id(0)
+
+    @pl.when(step == 0)
+    def _():
+        for lane, ids_ref in enumerate((token_ref, next_ref)):
+            slot, local = slots_of_row(ids_ref[...], rows_own, places, 2 * tokens // places)
+            slot_ref[2 * lane : 2 * lane + 1] = slot
+            slot_ref[2 * lane + 1 : 2 * lane + 2] = local
+
+    tags = jnp.zeros((rows, LANES), F32)
+    for lane in range(2):
+        slot, local = slot_ref[2 * lane : 2 * lane + 1], slot_ref[2 * lane + 1 : 2 * lane + 2]
+        chosen = (iota((rows, tokens), 0) + step * rows == slot).astype(BF16)
         if lane == 0:
             out_ref[:, :width] = jnp.dot(chosen, grad_ref[...], preferred_element_type=F32).astype(BF16)
         marks = jnp.where(iota((LANES, tokens), 0) == lane, local + 1, 0).astype(F32).astype(BF16)
         tags += lax.dot_general(chosen, marks, (((1,), (1,)), ((), ())), preferred_element_type=F32)
     out_ref[:, width:] = tags.astype(BF16)
+
+
+def pack(places, rows_own, token_ids, next_ids, embed_grad, pieces=4):
+    tokens, width = embed_grad.shape
+    slots, total = 2 * tokens, width + LANES
+    whole = lambda shape: pl.BlockSpec(shape, lambda i: (0, 0))
+    return pl.pallas_call(
+        functools.partial(pack_body, places, rows_own),
+        grid=(pieces,),
+        out_shape=jax.ShapeDtypeStruct((slots, total), BF16),
+        in_specs=[whole((1, tokens)), whole((1, tokens)), whole((tokens, width))],
+        out_specs=pl.BlockSpec((slots // pieces, total), lambda i: (i, 0)),
+        scratch_shapes=[pltpu.VMEM((8, tokens), I32)],
+        name="pack",
+        compiler_params=pltpu.CompilerParams(vmem_limit_bytes=60 << 20),
+        cost_estimate=pl.CostEstimate(flops=2 * slots * tokens * width, bytes_accessed=4 << 20, transcendentals=0),
+    )(token_ids.reshape(1, -1), next_ids.reshape(1, -1), embed_grad)
 
 
 def chosen_rows(got_ref, lane, width, rows, half_ref):
@@ -122,30 +147,28 @@
     out_ref[...] = jnp.dot(route_ref[...], replies_ref[...], preferred_element_type=F32).astype(BF16)
 
 
-def join_body(ranks, me_ref, own_ref, *refs):
-    ups, downs = refs[: ranks - 1], refs[ranks - 1 : 2 * ranks - 2]
-    out_ref, sems = refs[-2:]
+def join_body(ranks, me_ref, own_ref, up_ref, down_ref, up2_ref, down2_ref, far_ref, out_ref, sems):
     me = me_ref[0]
+    last = ranks - 1
     width = own_ref.shape[1]
-
-    def copy(src, rank, sem):
-        columns = pl.ds(pl.multiple_of(rank * width, LANES), width)
-        return pltpu.make_async_copy(src, out_ref.at[:, columns], sems.at[sem])
-
-    copies = [(None, copy(own_ref, me, 0))]
-    for k in range(1, ranks):
-        copies.append((me >= k, copy(ups[k - 1], jnp.maximum(me - k, 0), k)))
-        copies.append((me + k < ranks, copy(downs[k - 1], jnp.minimum(me + k, ranks - 1), ranks - 1 + k)))
-    for cond, c in copies:
-        if cond is None:
-            c.start()
-        else:
-            pl.when(cond)(c.start)
-    for cond, c in copies:
-        if cond is None:
-            c.wait()
-        else:
-            pl.when(cond)(c.wait)
+    plan = (
+        (own_ref, me, None),
+        (up_ref, me - 1, me >= 1),
+        (down_ref, me + 1, me < last),
+        (up2_ref, me - 2, me >= 2),
+        (down2_ref, me + 2, me < last - 1),
+        (far_ref, last - me, (me == 0) | (me == last)),
+    )
+    copies = []
+    for i, (src, rank, cond) in enumerate(plan):
+        start = pl.multiple_of(jnp.clip(rank, 0, last) * width, LANES)
+        copies.append((cond, pltpu.make_async_copy(src, out_ref.at[:, pl.ds(start, width)], sems.at[i])))
+    for method in ("start", "wait"):
+        for cond, c in copies:
+            if cond is None:
+                getattr(c, method)()
+            else:
+                pl.when(cond)(getattr(c, method))
 
 
 def on_device(param, moment_one, moment_two, proj_grad, embed_grad, token_ids, next_ids):
@@ -158,10 +181,7 @@
     half = lax.axis_index("zh").reshape(1)
     me = lax.axis_index("tp").reshape(1)
 
-    packed = call(
-        functools.partial(pack_body, places, rows_own), sds((slots, width + LANES), BF16), 3,
-        cost=(2 * slots * tokens * width, 4 << 20), name="pack",
-    )(token_ids.reshape(1, -1), next_ids.reshape(1, -1), embed_grad)
+    packed = pack(places, rows_own, token_ids, next_ids, embed_grad)
     got = lax.all_to_all(
         packed.reshape(places, slots // places, width + LANES), PLANE, split_axis=0, concat_axis=0, tiled=True
     ).reshape(slots, width + LANES)
@@ -183,29 +203,38 @@
         adam_body, (block, block, block, sds((rows_own, width), BF16)), 6,
         cost=(20 * rows_own * width, 2 << 20), name="adam",
     )(param, moment_one, moment_two, proj_grad, mine, theirs)
-    table_other = lax.ppermute(table, "zh", PAIR)
-    found = call(
-        find_body, sds((slots, width), BF16), 3, cost=(4 * slots * rows_own * width, 3 << 20), name="find",
-    )(chosen, table, table_other)
-    replies = lax.all_to_all(
-        found.reshape(places, slots // places, width), PLANE, split_axis=0, concat_axis=0, tiled=True
-    ).reshape(slots, width)
-    own = call(
-        pick_body, sds((tokens, width), BF16), 2, cost=(2 * slots * tokens * width, 4 << 20), name="pick",
-    )(route, replies)
-    ups, downs = [], []
-    up = down = own
-    for k in range(1, ranks):
-        up = lax.ppermute(up, "tp", [(i, i + 1) for i in range(k - 1, ranks - 1)])
-        down = lax.ppermute(down, "tp", [(i, i - 1) for i in range(1, ranks - k + 1)])
-        ups.append(up)
-        downs.append(down)
+
+    def reply(table, table_other):
+        found = call(
+            find_body, sds((slots, width), BF16), 3, cost=(4 * slots * rows_own * width, 3 << 20), name="find",
+        )(chosen, table, table_other)
+        return lax.all_to_all(
+            found.reshape(places, slots // places, width), PLANE, split_axis=0, concat_axis=0, tiled=True
+        ).reshape(slots, width)
+
+    def pick(replies):
+        return call(
+            pick_body, sds((tokens, width), BF16), 2, cost=(2 * slots * tokens * width, 4 << 20), name="pick",
+        )(route, replies)
+
+    replies = reply(table, lax.ppermute(table, "zh", PAIR))
+    last = ranks - 1
+    far = lax.ppermute(table, "tp", [(0, last), (last, 0)])
+    far_other = lax.ppermute(
+        table, ("zh", "tp"), [(last, ranks), (ranks, last), (ranks + last, 0), (0, ranks + last)]
+    )
+    far_replies = reply(far, far_other)
+    own = pick(replies)
+    steps = range(ranks)
+    up = lax.ppermute(own, "tp", [(i, i + 1) for i in steps[:-1]])
+    down = lax.ppermute(own, "tp", [(i, i - 1) for i in steps[1:]])
+    up2 = lax.ppermute(up, "tp", [(i, i + 1) for i in steps[1:-1]])
+    down2 = lax.ppermute(down, "tp", [(i, i - 1) for i in steps[1:-1]])
     next_rows = call(
         functools.partial(join_body, ranks), sds((tokens, ranks * width), BF16), 0,
-        specs=[SMEM] + [ANY] * (2 * ranks - 1), out_specs=ANY,
-        scratch=[pltpu.SemaphoreType.DMA((2 * ranks - 1,))],
+        specs=[SMEM] + [VMEM] * 6, out_specs=ANY, scratch=[pltpu.SemaphoreType.DMA((6,))],
         cost=(0, 8 << 20), name="join",
-    )(me, own, *ups, *downs)
+    )(me, own, up, down, up2, down2, pick(far_replies))
     return (new_param, new_one, new_two, next_rows)
 
 

time: 239 us -> 169 us (0.71)
  Pallas kernels: 66.1 us -> 20 us
  waiting for transfers between devices: 137 us -> 102 us
  starting transfers between devices: 27.7 us -> 41.6 us
    pallas_call x1, Pallas kernels: 56.7 us -> 3.89 us  [on_device(): call(functools.partial(join_body, ranks), sds((tokens, ranks * width), BF...]
    ppermute x7, waiting for transfers between devices: 76.7 us -> 54.2 us  [the longest x1 20.9 us: on_device(): up2 = lax.ppermute(up, 'tp', [(i, i + 1) for i in steps[1:-1]])]
    all_to_all x1 -> x2, waiting for transfers between devices: 21.5 us -> 8.44 us  [reply(): lax.all_to_all(found.reshape(places, slots // places, width), PLANE, spli...]
    all_to_all x1 -> x2, starting transfers between devices: 8.32 us -> 16.5 us  [reply(): lax.all_to_all(found.reshape(places, slots // places, width), PLANE, spli...]
    pallas_call x3 -> x5, Pallas kernels: 6.38 us -> 13.1 us  [the longest x2 5.77 us: reply(): call(find_body, sds((slots, width), BF16), 3, cost=(4 * slots * rows_own...]
    ppermute x7, starting transfers between devices: 10.3 us -> 16 us  [the longest x1 5.03 us: on_device(): down = lax.ppermute(own, 'tp', [(i, i - 1) for i in steps[1:]])]
    unnamed x22 -> x18, local copies, waits for them, and re-layouts: 5.98 us -> 3.68 us
  transfers between devices with their start and end apart: 10 -> 11, of which waited for: 8 -> 9; matrix products, arithmetic and copies ran while one was open for 0% -> 0% of each run, Pallas kernels for 1% -> 4%
where the time goes in v2:
time: 169 us; the launch traced here: 168 us
  waiting for transfers between devices  102 us (60%)
  starting transfers between devices  41.6 us (25%)
  Pallas kernels  20 us (12%)
  local copies, waits for them, and re-layouts  3.82 us (2%)
    all_to_all x1, waiting for transfers between devices, on_device(): lax.all_to_all(packed.reshape(places, slots // places, width + LANES), PL...  25.4 us
    ppermute x1, waiting for transfers between devices, on_device(): up2 = lax.ppermute(up, 'tp', [(i, i + 1) for i in steps[1:-1]])  20.9 us
    ppermute x1, waiting for transfers between devices, on_device(): down = lax.ppermute(own, 'tp', [(i, i - 1) for i in steps[1:]])  16.7 us
    all_to_all x2, starting transfers between devices, reply(): lax.all_to_all(found.reshape(places, slots // places, width), PLANE, spli...  16.5 us
    ppermute x1, waiting for transfers between devices, on_device(): theirs = lax.ppermute(other, 'zh', PAIR)  13.7 us
    ppermute x1, waiting for transfers between devices, on_device(): replies = reply(table, lax.ppermute(table, 'zh', PAIR))  10.2 us
    all_to_all x2, waiting for transfers between devices, reply(): lax.all_to_all(found.reshape(places, slots // places, width), PLANE, spli...  8.44 us
    all_to_all x1, starting transfers between devices, on_device(): lax.all_to_all(packed.reshape(places, slots // places, width + LANES), PL...  7.55 us
  transfers between devices with their start and end apart: 11, of which 9 were waited for; matrix products, arithmetic and copies ran while one was open for 0% of the time, Pallas kernels for 4%

profile of v2, /device:TPU:230, one launch (start us, length us, event | category | flops | bytes accessed | tf_op | source)
XLA Modules:
  0.0 167.9 jit_solution(10264196992052655267)
XLA Ops:
  0.6 4.9 %pack.1 = bf16[1024,1024]{1,0:T(8,128)(2,1)} custom-call(s32[1,512]{1,0:T(1,128)} %bitcast.18, s32[1,512]{1,0:T(1,128)} %bitcast.16, bf16[512,896]{1,0:T(8,128)(2,1)} %grad_ref.1), custom_call_target="tpu_custom_call" | custom-call | flops 939524096 | bytes 4194304 | tf_op jit(solution)/shard_map/pack/pallas_call | solution.py:80
  5.5 7.6 %all-to-all-start = ((bf16[32,32,1024]{2,1,0:T(8,128)(2,1)}), bf16[32,32,1024]{2,1,0:T(8,128)(2,1)S(1)}, u32[]{:S(2)}, u32[]{:S(2)}) async-start(bf16[32,32,1024]{2,1,0:T(8,128)(2,1)} %bitcast.15), calls=%async_computation | async-start | bytes 4194304 | tf_op jit(solution)/shard_map/all_to_all | solution.py:185
  13.1 25.4 %all-to-all-done = bf16[32,32,1024]{2,1,0:T(8,128)(2,1)S(1)} async-done(((bf16[32,32,1024]{2,1,0:T(8,128)(2,1)}), bf16[32,32,1024]{2,1,0:T(8,128)(2,1)S(1)}, u32[]{:S(2)}, u32[]{:S(2)}) %all-to-all-start) | async-done | bytes 2097184 | tf_op jit(solution)/shard_map/all_to_all | solution.py:185
  38.5 0.7 sum.1
  39.2 1.5 collective-permute-start
  40.8 13.7 %collective-permute-done.other_ref = f32[64,896]{1,0:T(8,128)S(1)} collective-permute-done((f32[64,896]{1,0:T(8,128)S(1)}, f32[64,896]{1,0:T(8,128)S(1)}, u32[]{:S(2)}, u32[]{:S(2)}) %collective-permute-start) | collective-permute-done | bytes 229408 | tf_op jit(solution)/shard_map/ppermute | solution.py:196
  54.5 1.0 adam.1
  55.4 0.2 ask.1.chosen_ref
  55.6 10.2 %collective-permute-done.1.other_ref = bf16[64,896]{1,0:T(8,128)(2,1)S(1)} collective-permute-done((bf16[64,896]{1,0:T(8,128)(2,1)S(1)}, bf16[64,896]{1,0:T(8,128)(2,1)S(1)}, u32[]{:S(2)}, u32[]{:S(2)}) %collective-permute-start.1) | collective-permute-done | bytes 114720 | tf_op jit(solution)/shard_map/ppermute | solution.py:220
  65.9 2.4 %find.2 = bf16[1024,896]{1,0:T(8,128)(2,1)} custom-call(bf16[1024,128]{1,0:T(8,128)(2,1)S(1)} %ask.1.chosen_ref, bf16[64,896]{1,0:T(8,128)(2,1)S(1)} %get-tuple-element.15.mine_ref, bf16[64,896]{1,0:T(8,128)(2,1)S(1)} %collective-permute-done.1.other_ref), custom_call_target="tpu_custom_call" | custom-call | flops 234881024 | bytes 3145728 | tf_op jit(solution)/shard_map/find/pallas_call | solution.py:208
  68.3 8.3 %all-to-all-start.1 = ((bf16[32,32,896]{2,1,0:T(8,128)(2,1)}), bf16[32,32,896]{2,1,0:T(8,128)(2,1)S(1)}, u32[]{:S(2)}, u32[]{:S(2)}) async-start(bf16[32,32,896]{2,1,0:T(8,128)(2,1)} %bitcast.7), calls=%async_computation.1 | async-start | bytes 3670016 | tf_op jit(solution)/shard_map/all_to_all | solution.py:211
  76.6 1.9 %collective-permute-start.7 = (bf16[64,896]{1,0:T(8,128)(2,1)S(1)}, bf16[64,896]{1,0:T(8,128)(2,1)}, u32[]{:S(2)}, u32[]{:S(2)}) collective-permute-start(bf16[64,896]{1,0:T(8,128)(2,1)S(1)} %get-tuple-element.15.mine_ref), channel_id=1, source_target_pairs={{3,128},{128,3},{131,0},{0,131},{7,132},{132,7},{135,4},{4,135},{1... | collective-permute-start | bytes 344072 | tf_op jit(solution)/shard_map/ppermute | solution.py:223
  78.5 4.9 %collective-permute-start.6 = (bf16[64,896]{1,0:T(8,128)(2,1)S(1)}, bf16[64,896]{1,0:T(8,128)(2,1)}, u32[]{:S(2)}, u32[]{:S(2)}) collective-permute-start(bf16[64,896]{1,0:T(8,128)(2,1)S(1)} %get-tuple-element.15.mine_ref), channel_id=1, source_target_pairs={{0,3},{3,0},{4,7},{7,4},{8,11},{11,8},{12,15},{15,12},{16,19},{19,... | collective-permute-start | bytes 344072 | tf_op jit(solution)/shard_map/ppermute | solution.py:222
  83.6 1.1 route.1.route_ref
  84.7 0.3 collective-permute-done.7.other_ref
  84.9 2.5 %collective-permute-done.6.mine_ref = bf16[64,896]{1,0:T(8,128)(2,1)} collective-permute-done((bf16[64,896]{1,0:T(8,128)(2,1)S(1)}, bf16[64,896]{1,0:T(8,128)(2,1)}, u32[]{:S(2)}, u32[]{:S(2)}) %collective-permute-start.6) | collective-permute-done | bytes 114720 | tf_op jit(solution)/shard_map/ppermute | solution.py:222
  87.5 3.4 %find.3 = bf16[1024,896]{1,0:T(8,128)(2,1)} custom-call(bf16[1024,128]{1,0:T(8,128)(2,1)S(1)} %ask.1.chosen_ref, bf16[64,896]{1,0:T(8,128)(2,1)} %collective-permute-done.6.mine_ref, bf16[64,896]{1,0:T(8,128)(2,1)} %collective-permute-done.7.other_ref), custom_call_target="tpu_custom_call" | custom-call | flops 234881024 | bytes 3145728 | tf_op jit(solution)/shard_map/find/pallas_call | solution.py:208
  90.8 8.4 %all-to-all-done.1 = bf16[32,32,896]{2,1,0:T(8,128)(2,1)S(1)} async-done(((bf16[32,32,896]{2,1,0:T(8,128)(2,1)}), bf16[32,32,896]{2,1,0:T(8,128)(2,1)S(1)}, u32[]{:S(2)}, u32[]{:S(2)}) %all-to-all-start.1) | async-done | bytes 1835040 | tf_op jit(solution)/shard_map/all_to_all | solution.py:211
  99.3 1.2 copy-done
  100.5 8.2 %all-to-all-start.2 = ((bf16[32,32,896]{2,1,0:T(8,128)(2,1)}), bf16[32,32,896]{2,1,0:T(8,128)(2,1)S(1)}, u32[]{:S(2)}, u32[]{:S(2)}) async-start(bf16[32,32,896]{2,1,0:T(8,128)(2,1)} %bitcast.9), calls=%async_computation.2 | async-start | bytes 3670016 | tf_op jit(solution)/shard_map/all_to_all | solution.py:211
  108.7 1.5 copy-done.1
  110.2 1.2 pick.2.own_ref
  111.5 5.0 %collective-permute-start.3 = (bf16[512,896]{1,0:T(8,128)(2,1)S(1)}, bf16[512,896]{1,0:T(8,128)(2,1)}, u32[]{:S(2)}, u32[]{:S(2)}) collective-permute-start(bf16[512,896]{1,0:T(8,128)(2,1)S(1)} %pick.2.own_ref), channel_id=1, source_target_pairs={{1,0},{2,1},{3,2},{5,4},{6,5},{7,6},{9,8},{10,9},{11,10},{13,12},{... | collective-permute-start | bytes 2752520 | tf_op jit(solution)/shard_map/ppermute | solution.py:230
  116.5 1.3 collective-permute-start.2
  117.8 0.9 copy-done.2
  118.7 16.7 %collective-permute-done.3.down_ref = bf16[512,896]{1,0:T(8,128)(2,1)} collective-permute-done((bf16[512,896]{1,0:T(8,128)(2,1)S(1)}, bf16[512,896]{1,0:T(8,128)(2,1)}, u32[]{:S(2)}, u32[]{:S(2)}) %collective-permute-start.3) | collective-permute-done | bytes 917536 | tf_op jit(solution)/shard_map/ppermute | solution.py:230
  135.5 1.6 collective-permute-start.5
  137.1 3.5 %collective-permute-done.2.up_ref = bf16[512,896]{1,0:T(8,128)(2,1)} collective-permute-done((bf16[512,896]{1,0:T(8,128)(2,1)S(1)}, bf16[512,896]{1,0:T(8,128)(2,1)}, u32[]{:S(2)}, u32[]{:S(2)}) %collective-permute-start.2) | collective-permute-done | bytes 917536 | tf_op jit(solution)/shard_map/ppermute | solution.py:229
  140.6 1.3 collective-permute-start.4
  141.9 1.2 pick.3.far_ref
  143.2 20.9 %collective-permute-done.4.up2_ref = bf16[512,896]{1,0:T(8,128)(2,1)} collective-permute-done((bf16[512,896]{1,0:T(8,128)(2,1)}, bf16[512,896]{1,0:T(8,128)(2,1)}, u32[]{:S(2)}, u32[]{:S(2)}) %collective-permute-start.4) | collective-permute-done | bytes 917536 | tf_op jit(solution)/shard_map/ppermute | solution.py:231
  164.0 3.9 %join.1 = bf16[512,3584]{1,0:T(8,128)(2,1)} custom-call(s32[1]{0:T(128)} %bitcast.5.me_ref, bf16[512,896]{1,0:T(8,128)(2,1)S(1)} %copy-done.3, bf16[512,896]{1,0:T(8,128)(2,1)} %collective-permute-done.2.up_ref, bf16[512,896]{1,0:T(8,128)(2,1)} %collective-permute-done.3.down_ref, bf16[512,896]{1,0:T(8,128)(2,1)} %collective-permute-done.4.up2_ref, ...), custom_call_target="tpu_custom_call" | custom-call | bytes 8388608 | tf_op jit(solution)/shard_map/join/pallas_call | solution.py:233
  (19 shorter events, 0.2 us)
Async XLA Ops:
  5.5 33.0 %all-to-all-start = ((bf16[32,32,1024]{2,1,0:T(8,128)(2,1)}), bf16[32,32,1024]{2,1,0:T(8,128)(2,1)S(1)}, u32[]{:S(2)}, u32[]{:S(2)}) async-start(bf16[32,32,1024]{2,1,0:T(8,128)(2,1)} %bitcast.15), calls=%async_computation | async-start | bytes 4194304 | tf_op jit(solution)/shard_map/all_to_all | solution.py:185
  13.1 41.4 %copy-start.4 = (f32[64,896]{1,0:T(8,128)S(1)}, f32[64,896]{1,0:T(8,128)}, u32[]{:S(2)}) copy-start(f32[64,896]{1,0:T(8,128)} %param_ref.1) | copy-start | bytes 688132
  13.1 41.4 %copy-start.5 = (f32[64,896]{1,0:T(8,128)S(1)}, f32[64,896]{1,0:T(8,128)}, u32[]{:S(2)}) copy-start(f32[64,896]{1,0:T(8,128)} %one_ref.1) | copy-start | bytes 688132
  13.1 41.4 %copy-start.6 = (f32[64,896]{1,0:T(8,128)S(1)}, f32[64,896]{1,0:T(8,128)}, u32[]{:S(2)}) copy-start(f32[64,896]{1,0:T(8,128)} %two_ref.1) | copy-start | bytes 688132
  13.1 41.4 %copy-start.7 = (f32[64,896]{1,0:T(8,128)S(1)}, f32[64,896]{1,0:T(8,128)}, u32[]{:S(2)}) copy-start(f32[64,896]{1,0:T(8,128)} %proj_ref.1) | copy-start | bytes 688132
  39.2 15.2 %collective-permute-start = (f32[64,896]{1,0:T(8,128)S(1)}, f32[64,896]{1,0:T(8,128)S(1)}, u32[]{:S(2)}, u32[]{:S(2)}) collective-permute-start(f32[64,896]{1,0:T(8,128)S(1)} %get-tuple-element.11), channel_id=1, source_target_pairs={{0,128},{128,0},{1,129},{129,1},{2,130},{130,2},{3,131},{131,3},{4... | collective-permute-start | bytes 688136 | tf_op jit(solution)/shard_map/ppermute | solution.py:196
  55.4 10.5 %collective-permute-start.1 = (bf16[64,896]{1,0:T(8,128)(2,1)S(1)}, bf16[64,896]{1,0:T(8,128)(2,1)S(1)}, u32[]{:S(2)}, u32[]{:S(2)}) collective-permute-start(bf16[64,896]{1,0:T(8,128)(2,1)S(1)} %get-tuple-element.15.mine_ref), channel_id=1, source_target_pairs={{0,128},{128,0},{1,129},{129,1},{2,130},{130,2},{3,131},{131,3},{4... | collective-permute-start | bytes 344072 | tf_op jit(solution)/shard_map/ppermute | solution.py:220
  68.3 15.1 %copy-start.8 = (s32[512]{0:T(512)S(1)}, s32[512]{0:T(512)}, u32[]{:S(2)}) copy-start(s32[512]{0:T(512)} %param.13) | copy-start | bytes 6148
  68.3 31.0 %all-to-all-start.1 = ((bf16[32,32,896]{2,1,0:T(8,128)(2,1)}), bf16[32,32,896]{2,1,0:T(8,128)(2,1)S(1)}, u32[]{:S(2)}, u32[]{:S(2)}) async-start(bf16[32,32,896]{2,1,0:T(8,128)(2,1)} %bitcast.7), calls=%async_computation.1 | async-start | bytes 3670016 | tf_op jit(solution)/shard_map/all_to_all | solution.py:211
  76.6 8.4 %collective-permute-start.7 = (bf16[64,896]{1,0:T(8,128)(2,1)S(1)}, bf16[64,896]{1,0:T(8,128)(2,1)}, u32[]{:S(2)}, u32[]{:S(2)}) collective-permute-start(bf16[64,896]{1,0:T(8,128)(2,1)S(1)} %get-tuple-element.15.mine_ref), channel_id=1, source_target_pairs={{3,128},{128,3},{131,0},{0,131},{7,132},{132,7},{135,4},{4,135},{1... | collective-permute-start | bytes 344072 | tf_op jit(solution)/shard_map/ppermute | solution.py:223
  78.5 9.0 %collective-permute-start.6 = (bf16[64,896]{1,0:T(8,128)(2,1)S(1)}, bf16[64,896]{1,0:T(8,128)(2,1)}, u32[]{:S(2)}, u32[]{:S(2)}) collective-permute-start(bf16[64,896]{1,0:T(8,128)(2,1)S(1)} %get-tuple-element.15.mine_ref), channel_id=1, source_target_pairs={{0,3},{3,0},{4,7},{7,4},{8,11},{11,8},{12,15},{15,12},{16,19},{19,... | collective-permute-start | bytes 344072 | tf_op jit(solution)/shard_map/ppermute | solution.py:222
  99.3 1.2 copy-start
  100.5 41.4 %all-to-all-start.2 = ((bf16[32,32,896]{2,1,0:T(8,128)(2,1)}), bf16[32,32,896]{2,1,0:T(8,128)(2,1)S(1)}, u32[]{:S(2)}, u32[]{:S(2)}) async-start(bf16[32,32,896]{2,1,0:T(8,128)(2,1)} %bitcast.9), calls=%async_computation.2 | async-start | bytes 3670016 | tf_op jit(solution)/shard_map/all_to_all | solution.py:211
  108.7 1.5 copy-start.1
  111.5 24.0 %collective-permute-start.3 = (bf16[512,896]{1,0:T(8,128)(2,1)S(1)}, bf16[512,896]{1,0:T(8,128)(2,1)}, u32[]{:S(2)}, u32[]{:S(2)}) collective-permute-start(bf16[512,896]{1,0:T(8,128)(2,1)S(1)} %pick.2.own_ref), channel_id=1, source_target_pairs={{1,0},{2,1},{3,2},{5,4},{6,5},{7,6},{9,8},{10,9},{11,10},{13,12},{... | collective-permute-start | bytes 2752520 | tf_op jit(solution)/shard_map/ppermute | solution.py:230
  116.5 24.1 %collective-permute-start.2 = (bf16[512,896]{1,0:T(8,128)(2,1)S(1)}, bf16[512,896]{1,0:T(8,128)(2,1)}, u32[]{:S(2)}, u32[]{:S(2)}) collective-permute-start(bf16[512,896]{1,0:T(8,128)(2,1)S(1)} %pick.2.own_ref), channel_id=1, source_target_pairs={{0,1},{1,2},{2,3},{4,5},{5,6},{6,7},{8,9},{9,10},{10,11},{12,13},{... | collective-permute-start | bytes 2752520 | tf_op jit(solution)/shard_map/ppermute | solution.py:229
  117.8 0.9 copy-start.2
  135.5 7.7 %collective-permute-start.5 = (bf16[512,896]{1,0:T(8,128)(2,1)}, bf16[512,896]{1,0:T(8,128)(2,1)}, u32[]{:S(2)}, u32[]{:S(2)}) collective-permute-start(bf16[512,896]{1,0:T(8,128)(2,1)} %collective-permute-done.3.down_ref), channel_id=1, source_target_pairs={{1,0},{2,1},{5,4},{6,5},{9,8},{10,9},{13,12},{14,13},{17,16},{18,1... | collective-permute-start | bytes 2752520 | tf_op jit(solution)/shard_map/ppermute | solution.py:232
  140.6 23.4 %collective-permute-start.4 = (bf16[512,896]{1,0:T(8,128)(2,1)}, bf16[512,896]{1,0:T(8,128)(2,1)}, u32[]{:S(2)}, u32[]{:S(2)}) collective-permute-start(bf16[512,896]{1,0:T(8,128)(2,1)} %collective-permute-done.2.up_ref), channel_id=1, source_target_pairs={{1,2},{2,3},{5,6},{6,7},{9,10},{10,11},{13,14},{14,15},{17,18},{18... | collective-permute-start | bytes 2752520 | tf_op jit(solution)/shard_map/ppermute | solution.py:231
  141.9 22.1 %copy-start.3 = (bf16[512,896]{1,0:T(8,128)(2,1)S(1)}, bf16[512,896]{1,0:T(8,128)(2,1)}, u32[]{:S(2)}) copy-start(bf16[512,896]{1,0:T(8,128)(2,1)} %copy-done.2) | copy-start | bytes 2752516

commit v3 on v0

v3 whole, which is shorter than its diff:
```python
import functools

import jax
import jax.numpy as jnp
from jax import lax
from jax.experimental import pallas as pl
from jax.experimental.pallas import tpu as pltpu
from jax.sharding import Mesh, PartitionSpec as P

STEP = 1000
PLANE = ("y", "x", "c")
SECTION = ("zh",) + PLANE
PAIR = [(0, 1), (1, 0)]
LANES = 128
CHUNKS = (512, 384)
VMEM = pl.BlockSpec(memory_space=pltpu.VMEM)
SMEM = pl.BlockSpec(memory_space=pltpu.SMEM)
ANY = pl.BlockSpec(memory_space=pl.ANY)
BF16, F32, I32 = jnp.bfloat16, jnp.float32, jnp.int32
sds = jax.ShapeDtypeStruct


def iota(shape, dim):
    return lax.broadcasted_iota(I32, shape, dim)


def dot(a, b, dims=((1,), (0,))):
    return lax.dot_general(a, b, (dims, ((), ())), preferred_element_type=F32)


def params(vmem):
    return pltpu.CompilerParams(vmem_limit_bytes=vmem << 20)


def cost(flops, bytes_accessed):
    return pl.CostEstimate(flops=flops, bytes_accessed=bytes_accessed, transcendentals=0)


def call(body, out, specs, flops=0, moved=1 << 20, vmem=20, **more):
    return pl.pallas_call(
        body,
        out_shape=out,
        in_specs=specs,
        out_specs=more.pop("out_specs", jax.tree.map(lambda _: VMEM, out)),
        compiler_params=params(vmem),
        cost_estimate=cost(flops, moved),
        **more,
    )


def owner_slots(ids, half, rows_own, places, cap):
    tokens = ids.shape[1]
    owner = ids // rows_own
    hits = iota((2 * places, tokens), 0) == owner
    earlier = (iota((tokens, tokens), 0) < iota((tokens, tokens), 1)).astype(BF16)
    before = dot(hits.astype(BF16), earlier)
    rank = jnp.sum(jnp.where(hits, before, 0.0), axis=0, keepdims=True).astype(I32)
    slot = (owner % places) * cap + rank
    return slot, (owner // places != half).astype(I32), ids - owner * rows_own


def pack_body(group, places, rows_own, half_ref, token_ref, next_ref, grad_ref, out_ref, slot_ref):
    tokens, width = grad_ref.shape
    rows = out_ref.shape[0]
    step = pl.program_id(0)

    @pl.when(step == 0)
    def _():
        for i, ids_ref in enumerate((token_ref, next_ref)[: 1 + group]):
            slot, theirs, local = owner_slots(ids_ref[...], half_ref[0], rows_own, places, tokens // places)
            slot_ref[3 * i : 3 * i + 1] = jnp.where(theirs == group, slot, -1)
            slot_ref[3 * i + 1 : 3 * i + 2] = jnp.where(theirs == group, -1, slot)
            slot_ref[3 * i + 2 : 3 * i + 3] = local

    row = iota((rows, tokens), 0) + step * rows
    mine = (row == slot_ref[0:1]).astype(BF16)
    out_ref[:, :width] = dot(mine, grad_ref[...]).astype(BF16)
    if group:
        tags = jnp.zeros((rows, LANES), F32)
        for lane in range(4):
            at = 3 * (lane % 2)
            hits = mine if lane == 0 else (row == slot_ref[at + lane // 2 : at + lane // 2 + 1]).astype(BF16)
            marks = jnp.where(iota((LANES, tokens), 0) == lane, slot_ref[at + 2 : at + 3] + 1, 0)
            tags += dot(hits, marks.astype(F32).astype(BF16), ((1,), (1,)))
        out_ref[:, width:] = tags.astype(BF16)


def pack(group, places, rows_own, half, token_ids, next_ids, embed_grad, pieces=2):
    tokens, width = embed_grad.shape
    total = width + LANES * group
    whole = lambda shape: pl.BlockSpec(shape, lambda i: (0, 0))
    return pl.pallas_call(
        functools.partial(pack_body, group, places, rows_own),
        grid=(pieces,),
        out_shape=sds((tokens, total), BF16),
        in_specs=[SMEM, whole((1, tokens)), whole((1, tokens)), whole((tokens, width))],
        out_specs=pl.BlockSpec((tokens // pieces, total), lambda i: (i, 0)),
        scratch_shapes=[pltpu.VMEM((8, tokens), I32)],
        name="pack",
        compiler_params=params(60),
        cost_estimate=cost(2 * tokens * tokens * width, 3 << 20),
    )(half, token_ids.reshape(1, -1), next_ids.reshape(1, -1), embed_grad)


def chosen_rows(got_ref, lane, width, rows):
    tag = got_ref[:, width + lane : width + lane + 1].astype(F32).astype(I32) - 1
    return (tag == iota((got_ref.shape[0], rows), 1)).astype(F32).astype(BF16)


def sum_body(got_ref, out_ref):
    rows, width = out_ref.shape
    out_ref[...] = dot(chosen_rows(got_ref, 0, width, rows), got_ref[:, :width], ((0,), (0,)))


def tags_body(got_ref, *out_refs):
    for lane, ref in zip((1, 3), out_refs):
        ref[...] = chosen_rows(got_ref, lane, got_ref.shape[1] - LANES, ref.shape[1])


def adam_body(param_ref, one_ref, two_ref, proj_ref, tags_ref, got_ref, other_ref, p_ref, o_ref, t_ref, *table_refs):
    rows, width = param_ref.shape
    mine = dot(chosen_rows(tags_ref, 2, width, rows), got_ref[...], ((0,), (0,)))
    grad = proj_ref[...] + (mine + other_ref[...])
    one = 0.9 * one_ref[...] + 0.1 * grad
    two = 0.999 * two_ref[...] + 0.001 * grad * grad
    first_fix = 1.0 - 0.9**STEP
    second_fix = 1.0 - 0.999**STEP
    param = param_ref[...] - 0.01 * (one / first_fix) / (jnp.sqrt(two / second_fix) + 1e-08)
    o_ref[...] = one
    t_ref[...] = two
    p_ref[...] = param
    table = param.astype(BF16)
    at = 0
    for ref in table_refs[1:]:
        ref[...] = table[:, at : at + ref.shape[1]]
        at += ref.shape[1]
    table_refs[0][...] = table


def find_body(own_ask_ref, other_ask_ref, own_ref, other_ref, out_ref):
    places, slots, width = out_ref.shape
    cap = slots // 2
    for i, (ask_ref, table_ref) in enumerate(((own_ask_ref, own_ref), (other_ask_ref, other_ref))):
        found = dot(ask_ref[...], table_ref[...]).astype(BF16)
        out_ref[:, i * cap : (i + 1) * cap, :] = found.reshape(places, cap, width)


def route_body(places, rows_own, half_ref, ids_ref, out_ref):
    tokens, slots = out_ref.shape
    owner = ids_ref[...] // rows_own
    hits = iota((tokens, LANES), 1) == owner
    earlier = (iota((tokens, tokens), 1) < iota((tokens, tokens), 0)).astype(BF16)
    before = dot(earlier, hits.astype(BF16))
    rank = jnp.sum(jnp.where(hits, before, 0.0), axis=1, keepdims=True).astype(I32)
    theirs = (owner // places != half_ref[0]).astype(I32)
    slot = (2 * (owner % places) + theirs) * (tokens // places) + rank
    out_ref[...] = (iota((tokens, slots), 1) == slot).astype(BF16)


def pick_body(route_ref, replies_ref, out_ref):
    out_ref[...] = dot(route_ref[...], replies_ref[...]).astype(BF16)


def join_body(plan, ranks, width, fresh, me_ref, *refs):
    refs = refs if fresh else refs[1:]
    n = len(plan)
    sources, out_ref, buffers, sems = refs[:n], refs[n], refs[n + 1 : -1], refs[-1]
    me = me_ref[0]
    last = ranks - 1
    where = {
        "own": (me, None),
        "up": (me - 1, me >= 1),
        "down": (me + 1, me < last),
        "up2": (me - 2, me >= 2),
        "down2": (me + 2, me < last - 1),
        "far": (last - me, (me == 0) | (me == last)),
    }
    pieces = 4

    def act(cond, method):
        method() if cond is None else pl.when(cond)(method)

    loads, stores = [], []
    for i, (kind, at) in enumerate(plan):
        rank, cond = where[kind]
        rows, size = buffers[i].shape
        rows = rows // pieces
        start = pl.multiple_of(jnp.clip(rank, 0, last) * width + at, LANES)
        for k in range(pieces):
            part = pl.ds(k * rows, rows)
            staged = buffers[i].at[part]
            loads.append((cond, pltpu.make_async_copy(sources[i].at[part], staged, sems.at[0, i, k])))
            stores.append(
                (cond, pltpu.make_async_copy(staged, out_ref.at[part, pl.ds(start, size)], sems.at[1, i, k]))
            )
    for cond, load in loads:
        act(cond, load.start)
    for (cond, load), (_, store) in zip(loads, stores):
        act(cond, load.wait)
        act(cond, store.start)
    for cond, store in stores:
        act(cond, store.wait)


def join(me, ranks, width, out, pieces):
    tokens = pieces[0][2].shape[0]
    fresh = out is None
    arrays = [p[2] for p in pieces]
    return call(
        functools.partial(join_body, [p[:2] for p in pieces], ranks, width, fresh),
        sds((tokens, ranks * width), BF16),
        [SMEM] + [ANY] * (len(pieces) + (not fresh)),
        moved=2 << 20,
        out_specs=ANY,
        scratch_shapes=[pltpu.VMEM(x.shape, BF16) for x in arrays]
        + [pltpu.SemaphoreType.DMA((2, len(pieces), 4))],
        input_output_aliases={} if fresh else {1: 0},
    )(me, *(() if fresh else (out,)), *arrays)


def on_device(param, moment_one, moment_two, proj_grad, embed_grad, token_ids, next_ids):
    rows_own, width = param.shape
    places = lax.axis_size(PLANE)
    ranks = lax.axis_size("tp")
    tokens = token_ids.shape[0]
    cap = tokens // places
    last = ranks - 1
    half = lax.axis_index("zh").reshape(1)
    me = lax.axis_index("tp").reshape(1)

    def exchange(x):
        return lax.all_to_all(x, PLANE, split_axis=0, concat_axis=0, tiled=True)

    def dispatch(group):
        packed = pack(group, places, rows_own, half, token_ids, next_ids, embed_grad)
        total = packed.shape[1]
        return exchange(packed.reshape(places, cap, total)).reshape(tokens, total)

    tagged = dispatch(1)
    theirs = call(sum_body, sds((rows_own, width), F32), [VMEM], flops=2 * tokens * rows_own * width)(tagged)
    theirs = lax.ppermute(theirs, "zh", PAIR)
    got = dispatch(0)
    route = call(
        functools.partial(route_body, places, rows_own), sds((tokens, 2 * tokens), BF16), [SMEM, VMEM],
        flops=2 * tokens * tokens * LANES,
    )(half, next_ids.reshape(-1, 1))
    block = sds((rows_own, width), F32)
    tables = tuple(sds((rows_own, n), BF16) for n in (width,) + CHUNKS)
    new_param, new_one, new_two, table, *chunks = call(
        adam_body, (block, block, block) + tables, [VMEM] * 7, flops=2 * tokens * rows_own * width,
    )(param, moment_one, moment_two, proj_grad, tagged, got, theirs)
    ask_other, ask_own = call(tags_body, (sds((tokens, rows_own), BF16),) * 2, [VMEM])(tagged)

    def reply(own, other):
        n = own.shape[1]
        found = call(
            find_body, sds((places, 2 * cap, n), BF16), [VMEM] * 4, flops=4 * tokens * rows_own * n
        )(ask_own, ask_other, own, other)
        return exchange(found).reshape(2 * tokens, n)

    def pick(replies):
        n = replies.shape[1]
        return call(pick_body, sds((tokens, n), BF16), [VMEM] * 2, flops=4 * tokens * tokens * n)(route, replies)

    others = [lax.ppermute(c, "zh", PAIR) for c in chunks]
    far = lax.ppermute(table, "tp", [(0, last), (last, 0)])
    far_other = lax.ppermute(table, ("zh", "tp"), [(last, ranks), (ranks, last), (ranks + last, 0), (0, ranks + last)])
    owns = [pick(reply(c, o)) for c, o in zip(chunks, others)]
    far_replies = reply(far, far_other)
    steps = range(ranks)
    near, next_near, at = [], [], 0
    for own in owns:
        up = lax.ppermute(own, "tp", [(i, i + 1) for i in steps[:-1]])
        down = lax.ppermute(own, "tp", [(i, i - 1) for i in steps[1:]])
        up2 = lax.ppermute(up, "tp", [(i, i + 1) for i in steps[1:-1]])
        down2 = lax.ppermute(down, "tp", [(i, i - 1) for i in steps[1:-1]])
        near.append([("own", at, own), ("up", at, up), ("down", at, down)])
        next_near.append([("up2", at, up2), ("down2", at, down2)])
        at += own.shape[1]
    far_rows = pick(far_replies)
    out = join(me, ranks, width, None, near[0] + near[1])
    out = join(me, ranks, width, out, next_near[0])
    out = join(me, ranks, width, out, [("far", 0, far_rows)])
    out = join(me, ranks, width, out, next_near[1])
    return (new_param, new_one, new_two, out)


def solution(mesh):
    grid = Mesh(mesh.devices.reshape(2, 4, 4, 2, mesh.shape["tp"]), SECTION + ("tp",))
    block = P(SECTION, "tp")
    return jax.shard_map(
        on_device,
        mesh=grid,
        in_specs=(block,) * 5 + (P(SECTION),) * 2,
        out_specs=(block,) * 3 + (P(SECTION, None),),
        check_vma=False,
    )
```

time: 257 us -> 162 us (0.63)
  waiting for transfers between devices: 147 us -> 66.6 us
  Pallas kernels: 0 us -> 26.3 us
  local copies, waits for them, and re-layouts: 22.2 us -> 4 us
  between operations: 14.2 us -> 0.92 us
  other arithmetic: 7.61 us -> 0 us
    all_gather x1 -> x0, waiting for transfers between devices: 95.1 us -> none  [on_device(): next_rows = lax.all_gather(mine, 'tp', axis=1, tiled=True)]
    ppermute x0 -> x13, waiting for transfers between devices: none -> 40.8 us  [the longest x2 16.5 us: on_device(): others = [lax.ppermute(c, 'zh', PAIR) for c in chunks]]
    ppermute x0 -> x13, starting transfers between devices: none -> 28.7 us  [the longest x2 10.9 us: on_device(): down = lax.ppermute(own, 'tp', [(i, i - 1) for i in steps[1:]])]
    all_to_all x4 -> x5, starting transfers between devices: 62.7 us -> 34.6 us  [exchange(): return lax.all_to_all(x, PLANE, split_axis=0, concat_axis=0, tiled=True)]
    pallas_call x0 -> x16, Pallas kernels: none -> 26.3 us  [the longest x4 9.33 us: join(): call(functools.partial(join_body, [p[:2] for p in pieces], ranks, width,...]
    all_to_all x4 -> x5, waiting for transfers between devices: 51.7 us -> 25.8 us  [exchange(): return lax.all_to_all(x, PLANE, split_axis=0, concat_axis=0, tiled=True)]
    scatter x3 -> x0, local copies, waits for them, and re-layouts: 9.47 us -> none  [the longest x1 4.58 us: on_device(): jnp.zeros((owners * cap, width), jnp.bfloat16).at[slot].set(embed_grad)]
    gather x2 -> x0, local copies, waits for them, and re-layouts: 6.09 us -> none  [the longest x1 4.04 us: on_device(): jnp.take(table, jnp.clip(lax.all_to_all(asking, 'section', split_axis=0,...]
  transfers between devices with their start and end apart: 5 -> 18, of which waited for: 4 -> 15; matrix products, arithmetic and copies ran while one was open for 4% -> 0% of each run, Pallas kernels for 0% -> 11%
where the time goes in v3:
time: 162 us; the launch traced here: 161 us
  waiting for transfers between devices  66.6 us (41%)
  starting transfers between devices  63.3 us (39%)
  Pallas kernels  26.3 us (16%)
  local copies, waits for them, and re-layouts  4 us (2%)
    all_to_all x5, starting transfers between devices, exchange(): return lax.all_to_all(x, PLANE, split_axis=0, concat_axis=0, tiled=True)  34.6 us
    all_to_all x5, waiting for transfers between devices, exchange(): return lax.all_to_all(x, PLANE, split_axis=0, concat_axis=0, tiled=True)  25.8 us
    ppermute x2, waiting for transfers between devices, on_device(): others = [lax.ppermute(c, 'zh', PAIR) for c in chunks]  16.5 us
    ppermute x2, starting transfers between devices, on_device(): down = lax.ppermute(own, 'tp', [(i, i - 1) for i in steps[1:]])  10.9 us
    pallas_call x4, Pallas kernels, join(): call(functools.partial(join_body, [p[:2] for p in pieces], ranks, width,...  9.33 us
    ppermute x2, waiting for transfers between devices, on_device(): up = lax.ppermute(own, 'tp', [(i, i + 1) for i in steps[:-1]])  8.52 us
    ppermute x2, waiting for transfers between devices, on_device(): up2 = lax.ppermute(up, 'tp', [(i, i + 1) for i in steps[1:-1]])  7.41 us
    pallas_call x2, Pallas kernels, pack(): pl.pallas_call(functools.partial(pack_body, group, places, rows_own), gri...  6.92 us
  transfers between devices with their start and end apart: 18, of which 15 were waited for; matrix products, arithmetic and copies ran while one was open for 0% of the time, Pallas kernels for 11%

profile of v3, /device:TPU:230, one launch (start us, length us, event | category | flops | bytes accessed | tf_op | source)
XLA Modules:
  0.0 161.1 jit_solution(12149126889560272998)
XLA Ops:
  0.6 3.8 %pack.2 = bf16[512,1024]{1,0:T(8,128)(2,1)} custom-call(s32[1]{0:T(128)} %bitcast.half_ref, s32[1,512]{1,0:T(1,128)} %bitcast.24, s32[1,512]{1,0:T(1,128)} %bitcast.21, bf16[512,896]{1,0:T(8,128)(2,1)} %grad_ref.3), custom_call_target="tpu_custom_call" | custom-call | flops 469762048 | bytes 3145728 | tf_op jit(solution)/shard_map/pack/pallas_call | solution.py:92
  4.4 7.7 %all-to-all-start = ((bf16[32,16,1024]{2,1,0:T(8,128)(2,1)}), bf16[32,16,1024]{2,1,0:T(8,128)(2,1)S(1)}, u32[]{:S(2)}, u32[]{:S(2)}) async-start(bf16[32,16,1024]{2,1,0:T(8,128)(2,1)} %bitcast.19), calls=%async_computation | async-start | bytes 2097152 | tf_op jit(solution)/shard_map/all_to_all | solution.py:232
  12.1 3.1 %pack.3 = bf16[512,896]{1,0:T(8,128)(2,1)} custom-call(s32[1]{0:T(128)} %bitcast.half_ref, s32[1,512]{1,0:T(1,128)} %bitcast.25, s32[1,512]{1,0:T(1,128)} %bitcast.22, bf16[512,896]{1,0:T(8,128)(2,1)} %grad_ref.3), custom_call_target="tpu_custom_call" | custom-call | flops 469762048 | bytes 3145728 | tf_op jit(solution)/shard_map/pack/pallas_call | solution.py:92
  15.3 11.5 %all-to-all-done = bf16[32,16,1024]{2,1,0:T(8,128)(2,1)S(1)} async-done(((bf16[32,16,1024]{2,1,0:T(8,128)(2,1)}), bf16[32,16,1024]{2,1,0:T(8,128)(2,1)S(1)}, u32[]{:S(2)}, u32[]{:S(2)}) %all-to-all-start) | async-done | bytes 1048608 | tf_op jit(solution)/shard_map/all_to_all | solution.py:232
  26.7 6.4 %all-to-all-start.1 = ((bf16[32,16,896]{2,1,0:T(8,128)(2,1)}), bf16[32,16,896]{2,1,0:T(8,128)(2,1)S(1)}, u32[]{:S(2)}, u32[]{:S(2)}) async-start(bf16[32,16,896]{2,1,0:T(8,128)(2,1)} %bitcast.20), calls=%async_computation.1 | async-start | bytes 1835008 | tf_op jit(solution)/shard_map/all_to_all | solution.py:232
  33.6 1.5 collective-permute-start
  35.1 11.4 %all-to-all-done.1 = bf16[32,16,896]{2,1,0:T(8,128)(2,1)S(1)} async-done(((bf16[32,16,896]{2,1,0:T(8,128)(2,1)}), bf16[32,16,896]{2,1,0:T(8,128)(2,1)S(1)}, u32[]{:S(2)}, u32[]{:S(2)}) %all-to-all-start.1) | async-done | bytes 917536 | tf_op jit(solution)/shard_map/all_to_all | solution.py:232
  46.6 1.7 %collective-permute-done.other_ref = f32[64,896]{1,0:T(8,128)S(1)} collective-permute-done((f32[64,896]{1,0:T(8,128)S(1)}, f32[64,896]{1,0:T(8,128)S(1)}, u32[]{:S(2)}, u32[]{:S(2)}) %collective-permute-start) | collective-permute-done | bytes 229408 | tf_op jit(solution)/shard_map/ppermute | solution.py:241
  50.3 7.4 %collective-permute-done.4.other_ref = bf16[64,384]{1,0:T(8,128)(2,1)S(1)} collective-permute-done((bf16[64,384]{1,0:T(8,128)(2,1)S(1)}, bf16[64,384]{1,0:T(8,128)(2,1)S(1)}, u32[]{:S(2)}, u32[]{:S(2)}) %collective-permute-start.4) | collective-permute-done | bytes 49184 | tf_op jit(solution)/shard_map/ppermute | solution.py:265
  58.9 7.5 %all-to-all-start.3 = ((bf16[32,32,384]{2,1,0:T(8,128)(2,1)}), bf16[32,32,384]{2,1,0:T(8,128)(2,1)S(1)}, u32[]{:S(2)}, u32[]{:S(2)}) async-start(bf16[32,32,384]{2,1,0:T(8,128)(2,1)} %shard_map.108), calls=%async_computation.3 | async-start | bytes 1572864 | tf_op jit(solution)/shard_map/all_to_all | solution.py:232
  66.9 9.2 %collective-permute-done.1.other_ref = bf16[64,512]{1,0:T(8,128)(2,1)S(1)} collective-permute-done((bf16[64,512]{1,0:T(8,128)(2,1)S(1)}, bf16[64,512]{1,0:T(8,128)(2,1)S(1)}, u32[]{:S(2)}, u32[]{:S(2)}) %collective-permute-start.1) | collective-permute-done | bytes 65568 | tf_op jit(solution)/shard_map/ppermute | solution.py:265
  76.0 1.4 shard_map.106
  79.2 6.5 %all-to-all-start.2 = ((bf16[32,32,512]{2,1,0:T(8,128)(2,1)}), bf16[32,32,512]{2,1,0:T(8,128)(2,1)S(1)}, u32[]{:S(2)}, u32[]{:S(2)}) async-start(bf16[32,32,512]{2,1,0:T(8,128)(2,1)} %shard_map.106), calls=%async_computation.2 | async-start | bytes 2097152 | tf_op jit(solution)/shard_map/all_to_all | solution.py:232
  85.7 1.9 %collective-permute-start.10 = (bf16[64,896]{1,0:T(8,128)(2,1)S(1)}, bf16[64,896]{1,0:T(8,128)(2,1)S(1)}, u32[]{:S(2)}, u32[]{:S(2)}) collective-permute-start(bf16[64,896]{1,0:T(8,128)(2,1)S(1)} %get-tuple-element.19), channel_id=1, source_target_pairs={{3,128},{128,3},{131,0},{0,131},{7,132},{132,7},{135,4},{4,135},{1... | collective-permute-start | bytes 344072 | tf_op jit(solution)/shard_map/ppermute | solution.py:267
  87.6 5.4 %collective-permute-start.9 = (bf16[64,896]{1,0:T(8,128)(2,1)S(1)}, bf16[64,896]{1,0:T(8,128)(2,1)S(1)}, u32[]{:S(2)}, u32[]{:S(2)}) collective-permute-start(bf16[64,896]{1,0:T(8,128)(2,1)S(1)} %get-tuple-element.19), channel_id=1, source_target_pairs={{0,3},{3,0},{4,7},{7,4},{8,11},{11,8},{12,15},{15,12},{16,19},{19,... | collective-permute-start | bytes 344072 | tf_op jit(solution)/shard_map/ppermute | solution.py:266
  93.9 2.5 %collective-permute-done.9.own_ref = bf16[64,896]{1,0:T(8,128)(2,1)S(1)} collective-permute-done((bf16[64,896]{1,0:T(8,128)(2,1)S(1)}, bf16[64,896]{1,0:T(8,128)(2,1)S(1)}, u32[]{:S(2)}, u32[]{:S(2)}) %collective-permute-start.9) | collective-permute-done | bytes 114720 | tf_op jit(solution)/shard_map/ppermute | solution.py:266
  96.5 1.9 %shard_map.112 = bf16[32,32,896]{2,1,0:T(8,128)(2,1)} custom-call(bf16[512,64]{1,0:T(8,128)(2,1)S(1)} %get-tuple-element.15.own_ask_ref, bf16[512,64]{1,0:T(8,128)(2,1)S(1)} %get-tuple-element.16.other_ask_ref, bf16[64,896]{1,0:T(8,128)(2,1)S(1)} %collective-permute-done.9.own_ref, bf16[64,896]{1,0:T(8,128)(2,1)S(1)} %collective-permute-done.10.other_ref), custom_call_target="tpu_custom_call" | custom-call | flops 117440512 | bytes 1048576 | tf_op jit(solution)/shard_map/pallas_call | solution.py:256
  98.3 2.0 %all-to-all-done.2 = bf16[32,32,512]{2,1,0:T(8,128)(2,1)S(1)} async-done(((bf16[32,32,512]{2,1,0:T(8,128)(2,1)}), bf16[32,32,512]{2,1,0:T(8,128)(2,1)S(1)}, u32[]{:S(2)}, u32[]{:S(2)}) %all-to-all-start.2) | async-done | bytes 1048608 | tf_op jit(solution)/shard_map/all_to_all | solution.py:232
  100.3 6.5 %all-to-all-start.4 = ((bf16[32,32,896]{2,1,0:T(8,128)(2,1)}), bf16[32,32,896]{2,1,0:T(8,128)(2,1)S(1)}, u32[]{:S(2)}, u32[]{:S(2)}) async-start(bf16[32,32,896]{2,1,0:T(8,128)(2,1)} %shard_map.112), calls=%async_computation.4 | async-start | bytes 3670016 | tf_op jit(solution)/shard_map/all_to_all | solution.py:232
  109.9 5.6 %collective-permute-start.3 = (bf16[512,512]{1,0:T(8,128)(2,1)S(1)}, bf16[512,512]{1,0:T(8,128)(2,1)}, u32[]{:S(2)}, u32[]{:S(2)}) collective-permute-start(bf16[512,512]{1,0:T(8,128)(2,1)S(1)} %shard_map.107.refs_0_), channel_id=1, source_target_pairs={{1,0},{2,1},{3,2},{5,4},{6,5},{7,6},{9,8},{10,9},{11,10},{13,12},{... | collective-permute-start | bytes 1572872 | tf_op jit(solution)/shard_map/ppermute | solution.py:274
  117.5 5.3 %collective-permute-start.6 = (bf16[512,384]{1,0:T(8,128)(2,1)S(1)}, bf16[512,384]{1,0:T(8,128)(2,1)}, u32[]{:S(2)}, u32[]{:S(2)}) collective-permute-start(bf16[512,384]{1,0:T(8,128)(2,1)S(1)} %shard_map.109.refs_3_), channel_id=1, source_target_pairs={{1,0},{2,1},{3,2},{5,4},{6,5},{7,6},{9,8},{10,9},{11,10},{13,12},{... | collective-permute-start | bytes 1179656 | tf_op jit(solution)/shard_map/ppermute | solution.py:274
  124.9 2.1 %collective-permute-done.3.refs_2_ = bf16[512,512]{1,0:T(8,128)(2,1)} collective-permute-done((bf16[512,512]{1,0:T(8,128)(2,1)S(1)}, bf16[512,512]{1,0:T(8,128)(2,1)}, u32[]{:S(2)}, u32[]{:S(2)}) %collective-permute-start.3) | collective-permute-done | bytes 524320 | tf_op jit(solution)/shard_map/ppermute | solution.py:274
  127.0 1.5 collective-permute-start.8
  128.5 3.8 %collective-permute-done.2.refs_1_ = bf16[512,512]{1,0:T(8,128)(2,1)} collective-permute-done((bf16[512,512]{1,0:T(8,128)(2,1)S(1)}, bf16[512,512]{1,0:T(8,128)(2,1)}, u32[]{:S(2)}, u32[]{:S(2)}) %collective-permute-start.2) | collective-permute-done | bytes 524320 | tf_op jit(solution)/shard_map/ppermute | solution.py:273
  134.6 1.4 collective-permute-start.12
  136.0 4.7 %collective-permute-done.5.refs_4_ = bf16[512,384]{1,0:T(8,128)(2,1)} collective-permute-done((bf16[512,384]{1,0:T(8,128)(2,1)S(1)}, bf16[512,384]{1,0:T(8,128)(2,1)}, u32[]{:S(2)}, u32[]{:S(2)}) %collective-permute-start.5) | collective-permute-done | bytes 393248 | tf_op jit(solution)/shard_map/ppermute | solution.py:273
  143.0 3.5 %shard_map.110.refs_0_ = bf16[512,3584]{1,0:T(8,128)(2,1)} custom-call(s32[1]{0:T(128)} %bitcast.7.me_ref, bf16[512,512]{1,0:T(8,128)(2,1)S(1)} %shard_map.107.refs_0_, bf16[512,512]{1,0:T(8,128)(2,1)} %collective-permute-done.2.refs_1_, bf16[512,512]{1,0:T(8,128)(2,1)} %collective-permute-done.3.refs_2_, bf16[512,384]{1,0:T(8,128)(2,1)S(1)} %copy-done.5, ...), custom_call_target="tpu_custom_call" | custom-call | bytes 2097152 | tf_op jit(solution)/shard_map/pallas_call | solution.py:209
  147.8 4.2 %collective-permute-done.7.refs_1_ = bf16[512,512]{1,0:T(8,128)(2,1)} collective-permute-done((bf16[512,512]{1,0:T(8,128)(2,1)}, bf16[512,512]{1,0:T(8,128)(2,1)}, u32[]{:S(2)}, u32[]{:S(2)}) %collective-permute-start.7) | collective-permute-done | bytes 524320 | tf_op jit(solution)/shard_map/ppermute | solution.py:275
  152.0 1.9 %shard_map.111.refs_0_ = bf16[512,3584]{1,0:T(8,128)(2,1)} custom-call(s32[1]{0:T(128)} %bitcast.7.me_ref, bf16[512,3584]{1,0:T(8,128)(2,1)} %shard_map.110.refs_0_, bf16[512,512]{1,0:T(8,128)(2,1)} %collective-permute-done.7.refs_1_, bf16[512,512]{1,0:T(8,128)(2,1)} %collective-permute-done.8.refs_2_), custom_call_target="tpu_custom_call", output_to_operand_aliasing={{}: (1, {})} | custom-call | bytes 2097152 | tf_op jit(solution)/shard_map/pallas_call | solution.py:209
  153.9 2.2 %shard_map.114.refs_0_ = bf16[512,3584]{1,0:T(8,128)(2,1)} custom-call(s32[1]{0:T(128)} %bitcast.7.me_ref, bf16[512,3584]{1,0:T(8,128)(2,1)} %shard_map.111.refs_0_, bf16[512,896]{1,0:T(8,128)(2,1)S(1)} %shard_map.113.refs_1_), custom_call_target="tpu_custom_call", output_to_operand_aliasing={{}: (1, {})} | custom-call | bytes 2097152 | tf_op jit(solution)/shard_map/pallas_call | solution.py:209
  156.1 3.2 %collective-permute-done.11.refs_1_ = bf16[512,384]{1,0:T(8,128)(2,1)} collective-permute-done((bf16[512,384]{1,0:T(8,128)(2,1)}, bf16[512,384]{1,0:T(8,128)(2,1)}, u32[]{:S(2)}, u32[]{:S(2)}) %collective-permute-start.11) | collective-permute-done | bytes 393248 | tf_op jit(solution)/shard_map/ppermute | solution.py:275
  159.3 1.8 %shard_map.115 = bf16[512,3584]{1,0:T(8,128)(2,1)} custom-call(s32[1]{0:T(128)} %bitcast.7.me_ref, bf16[512,3584]{1,0:T(8,128)(2,1)} %shard_map.114.refs_0_, bf16[512,384]{1,0:T(8,128)(2,1)} %collective-permute-done.11.refs_1_, bf16[512,384]{1,0:T(8,128)(2,1)} %collective-permute-done.12.refs_2_), custom_call_target="tpu_custom_call", output_to_operand_aliasing={{}: (1, {})} | custom-call | bytes 2097152 | tf_op jit(solution)/shard_map/pallas_call | solution.py:209
  (43 shorter events, 19.7 us)
Async XLA Ops:
  4.4 43.9 %copy-start.6 = (f32[64,896]{1,0:T(8,128)S(1)}, f32[64,896]{1,0:T(8,128)}, u32[]{:S(2)}) copy-start(f32[64,896]{1,0:T(8,128)} %param_ref.1) | copy-start | bytes 688132
  4.4 43.9 %copy-start.7 = (f32[64,896]{1,0:T(8,128)S(1)}, f32[64,896]{1,0:T(8,128)}, u32[]{:S(2)}) copy-start(f32[64,896]{1,0:T(8,128)} %one_ref.1) | copy-start | bytes 688132
  4.4 43.9 %copy-start.8 = (f32[64,896]{1,0:T(8,128)S(1)}, f32[64,896]{1,0:T(8,128)}, u32[]{:S(2)}) copy-start(f32[64,896]{1,0:T(8,128)} %two_ref.1) | copy-start | bytes 688132
  4.4 43.9 %copy-start.9 = (f32[64,896]{1,0:T(8,128)S(1)}, f32[64,896]{1,0:T(8,128)}, u32[]{:S(2)}) copy-start(f32[64,896]{1,0:T(8,128)} %proj_ref.1) | copy-start | bytes 688132
  4.4 22.3 %all-to-all-start = ((bf16[32,16,1024]{2,1,0:T(8,128)(2,1)}), bf16[32,16,1024]{2,1,0:T(8,128)(2,1)S(1)}, u32[]{:S(2)}, u32[]{:S(2)}) async-start(bf16[32,16,1024]{2,1,0:T(8,128)(2,1)} %bitcast.19), calls=%async_computation | async-start | bytes 2097152 | tf_op jit(solution)/shard_map/all_to_all | solution.py:232
  26.7 19.8 %all-to-all-start.1 = ((bf16[32,16,896]{2,1,0:T(8,128)(2,1)}), bf16[32,16,896]{2,1,0:T(8,128)(2,1)S(1)}, u32[]{:S(2)}, u32[]{:S(2)}) async-start(bf16[32,16,896]{2,1,0:T(8,128)(2,1)} %bitcast.20), calls=%async_computation.1 | async-start | bytes 1835008 | tf_op jit(solution)/shard_map/all_to_all | solution.py:232
  33.6 14.7 %collective-permute-start = (f32[64,896]{1,0:T(8,128)S(1)}, f32[64,896]{1,0:T(8,128)S(1)}, u32[]{:S(2)}, u32[]{:S(2)}) collective-permute-start(f32[64,896]{1,0:T(8,128)S(1)} %shard_map.102), channel_id=1, source_target_pairs={{0,128},{128,0},{1,129},{129,1},{2,130},{130,2},{3,131},{131,3},{4... | collective-permute-start | bytes 688136 | tf_op jit(solution)/shard_map/ppermute | solution.py:241
  49.6 8.0 %collective-permute-start.4 = (bf16[64,384]{1,0:T(8,128)(2,1)S(1)}, bf16[64,384]{1,0:T(8,128)(2,1)S(1)}, u32[]{:S(2)}, u32[]{:S(2)}) collective-permute-start(bf16[64,384]{1,0:T(8,128)(2,1)S(1)} %get-tuple-element.18.own_ref), channel_id=1, source_target_pairs={{0,128},{128,0},{1,129},{129,1},{2,130},{130,2},{3,131},{131,3},{4... | collective-permute-start | bytes 147464 | tf_op jit(solution)/shard_map/ppermute | solution.py:265
  58.9 19.4 %all-to-all-start.3 = ((bf16[32,32,384]{2,1,0:T(8,128)(2,1)}), bf16[32,32,384]{2,1,0:T(8,128)(2,1)S(1)}, u32[]{:S(2)}, u32[]{:S(2)}) async-start(bf16[32,32,384]{2,1,0:T(8,128)(2,1)} %shard_map.108), calls=%async_computation.3 | async-start | bytes 1572864 | tf_op jit(solution)/shard_map/all_to_all | solution.py:232
  66.3 9.7 %collective-permute-start.1 = (bf16[64,512]{1,0:T(8,128)(2,1)S(1)}, bf16[64,512]{1,0:T(8,128)(2,1)S(1)}, u32[]{:S(2)}, u32[]{:S(2)}) collective-permute-start(bf16[64,512]{1,0:T(8,128)(2,1)S(1)} %get-tuple-element.17.own_ref), channel_id=1, source_target_pairs={{0,128},{128,0},{1,129},{129,1},{2,130},{130,2},{3,131},{131,3},{4... | collective-permute-start | bytes 196616 | tf_op jit(solution)/shard_map/ppermute | solution.py:265
  77.4 29.4 %copy-start.10 = (s32[512]{0:T(512)S(1)}, s32[512]{0:T(512)}, u32[]{:S(2)}) copy-start(s32[512]{0:T(512)} %param.13) | copy-start | bytes 6148
  78.3 0.9 copy-start.2
  79.2 21.1 %all-to-all-start.2 = ((bf16[32,32,512]{2,1,0:T(8,128)(2,1)}), bf16[32,32,512]{2,1,0:T(8,128)(2,1)S(1)}, u32[]{:S(2)}, u32[]{:S(2)}) async-start(bf16[32,32,512]{2,1,0:T(8,128)(2,1)} %shard_map.106), calls=%async_computation.2 | async-start | bytes 2097152 | tf_op jit(solution)/shard_map/all_to_all | solution.py:232
  85.7 8.3 %collective-permute-start.10 = (bf16[64,896]{1,0:T(8,128)(2,1)S(1)}, bf16[64,896]{1,0:T(8,128)(2,1)S(1)}, u32[]{:S(2)}, u32[]{:S(2)}) collective-permute-start(bf16[64,896]{1,0:T(8,128)(2,1)S(1)} %get-tuple-element.19), channel_id=1, source_target_pairs={{3,128},{128,3},{131,0},{0,131},{7,132},{132,7},{135,4},{4,135},{1... | collective-permute-start | bytes 344072 | tf_op jit(solution)/shard_map/ppermute | solution.py:267
  87.6 8.9 %collective-permute-start.9 = (bf16[64,896]{1,0:T(8,128)(2,1)S(1)}, bf16[64,896]{1,0:T(8,128)(2,1)S(1)}, u32[]{:S(2)}, u32[]{:S(2)}) collective-permute-start(bf16[64,896]{1,0:T(8,128)(2,1)S(1)} %get-tuple-element.19), channel_id=1, source_target_pairs={{0,3},{3,0},{4,7},{7,4},{8,11},{11,8},{12,15},{15,12},{16,19},{19,... | collective-permute-start | bytes 344072 | tf_op jit(solution)/shard_map/ppermute | solution.py:266
  100.3 6.5 %copy-start = (bf16[32,32,512]{2,1,0:T(8,128)(2,1)}, bf16[32,32,512]{2,1,0:T(8,128)(2,1)S(1)}, u32[]{:S(2)}) copy-start(bf16[32,32,512]{2,1,0:T(8,128)(2,1)S(1)} %all-to-all-done.2) | copy-start | bytes 3145732
  100.3 46.2 %all-to-all-start.4 = ((bf16[32,32,896]{2,1,0:T(8,128)(2,1)}), bf16[32,32,896]{2,1,0:T(8,128)(2,1)S(1)}, u32[]{:S(2)}, u32[]{:S(2)}) async-start(bf16[32,32,896]{2,1,0:T(8,128)(2,1)} %shard_map.112), calls=%async_computation.4 | async-start | bytes 3670016 | tf_op jit(solution)/shard_map/all_to_all | solution.py:232
  107.0 9.8 %copy-start.3 = (bf16[32,32,384]{2,1,0:T(8,128)(2,1)S(1)}, bf16[32,32,384]{2,1,0:T(8,128)(2,1)}, u32[]{:S(2)}) copy-start(bf16[32,32,384]{2,1,0:T(8,128)(2,1)} %copy-done.2) | copy-start | bytes 2359300
  108.0 1.2 copy-start.1
  109.9 17.1 %collective-permute-start.3 = (bf16[512,512]{1,0:T(8,128)(2,1)S(1)}, bf16[512,512]{1,0:T(8,128)(2,1)}, u32[]{:S(2)}, u32[]{:S(2)}) collective-permute-start(bf16[512,512]{1,0:T(8,128)(2,1)S(1)} %shard_map.107.refs_0_), channel_id=1, source_target_pairs={{1,0},{2,1},{3,2},{5,4},{6,5},{7,6},{9,8},{10,9},{11,10},{13,12},{... | collective-permute-start | bytes 1572872 | tf_op jit(solution)/shard_map/ppermute | solution.py:274
  115.5 16.8 %collective-permute-start.2 = (bf16[512,512]{1,0:T(8,128)(2,1)S(1)}, bf16[512,512]{1,0:T(8,128)(2,1)}, u32[]{:S(2)}, u32[]{:S(2)}) collective-permute-start(bf16[512,512]{1,0:T(8,128)(2,1)S(1)} %shard_map.107.refs_0_), channel_id=1, source_target_pairs={{0,1},{1,2},{2,3},{4,5},{5,6},{6,7},{8,9},{9,10},{10,11},{12,13},{... | collective-permute-start | bytes 1572872 | tf_op jit(solution)/shard_map/ppermute | solution.py:273
  117.5 17.1 %collective-permute-start.6 = (bf16[512,384]{1,0:T(8,128)(2,1)S(1)}, bf16[512,384]{1,0:T(8,128)(2,1)}, u32[]{:S(2)}, u32[]{:S(2)}) collective-permute-start(bf16[512,384]{1,0:T(8,128)(2,1)S(1)} %shard_map.109.refs_3_), channel_id=1, source_target_pairs={{1,0},{2,1},{3,2},{5,4},{6,5},{7,6},{9,8},{10,9},{11,10},{13,12},{... | collective-permute-start | bytes 1179656 | tf_op jit(solution)/shard_map/ppermute | solution.py:274
  122.9 17.9 %collective-permute-start.5 = (bf16[512,384]{1,0:T(8,128)(2,1)S(1)}, bf16[512,384]{1,0:T(8,128)(2,1)}, u32[]{:S(2)}, u32[]{:S(2)}) collective-permute-start(bf16[512,384]{1,0:T(8,128)(2,1)S(1)} %shard_map.109.refs_3_), channel_id=1, source_target_pairs={{0,1},{1,2},{2,3},{4,5},{5,6},{6,7},{8,9},{9,10},{10,11},{12,13},{... | collective-permute-start | bytes 1179656 | tf_op jit(solution)/shard_map/ppermute | solution.py:273
  124.1 0.7 copy-start.4
  127.0 20.7 %collective-permute-start.8 = (bf16[512,512]{1,0:T(8,128)(2,1)}, bf16[512,512]{1,0:T(8,128)(2,1)}, u32[]{:S(2)}, u32[]{:S(2)}) collective-permute-start(bf16[512,512]{1,0:T(8,128)(2,1)} %collective-permute-done.3.refs_2_), channel_id=1, source_target_pairs={{1,0},{2,1},{5,4},{6,5},{9,8},{10,9},{13,12},{14,13},{17,16},{18,1... | collective-permute-start | bytes 1572872 | tf_op jit(solution)/shard_map/ppermute | solution.py:276
  132.3 19.7 %collective-permute-start.7 = (bf16[512,512]{1,0:T(8,128)(2,1)}, bf16[512,512]{1,0:T(8,128)(2,1)}, u32[]{:S(2)}, u32[]{:S(2)}) collective-permute-start(bf16[512,512]{1,0:T(8,128)(2,1)} %collective-permute-done.2.refs_1_), channel_id=1, source_target_pairs={{1,2},{2,3},{5,6},{6,7},{9,10},{10,11},{13,14},{14,15},{17,18},{18... | collective-permute-start | bytes 1572872 | tf_op jit(solution)/shard_map/ppermute | solution.py:275
  134.6 21.4 %collective-permute-start.12 = (bf16[512,384]{1,0:T(8,128)(2,1)}, bf16[512,384]{1,0:T(8,128)(2,1)}, u32[]{:S(2)}, u32[]{:S(2)}) collective-permute-start(bf16[512,384]{1,0:T(8,128)(2,1)} %collective-permute-done.6.refs_5_), channel_id=1, source_target_pairs={{1,0},{2,1},{5,4},{6,5},{9,8},{10,9},{13,12},{14,13},{17,16},{18,1... | collective-permute-start | bytes 1179656 | tf_op jit(solution)/shard_map/ppermute | solution.py:276
  140.7 18.5 %collective-permute-start.11 = (bf16[512,384]{1,0:T(8,128)(2,1)}, bf16[512,384]{1,0:T(8,128)(2,1)}, u32[]{:S(2)}, u32[]{:S(2)}) collective-permute-start(bf16[512,384]{1,0:T(8,128)(2,1)} %collective-permute-done.5.refs_4_), channel_id=1, source_target_pairs={{1,2},{2,3},{5,6},{6,7},{9,10},{10,11},{13,14},{14,15},{17,18},{18... | collective-permute-start | bytes 1179656 | tf_op jit(solution)/shard_map/ppermute | solution.py:275
  142.0 1.0 copy-start.5

commit v4 on v3

--- a/solution.py
+++ b/solution.py
@@ -48,15 +48,19 @@
     )
 
 
-def owner_slots(ids, half, rows_own, places, cap):
-    tokens = ids.shape[1]
-    owner = ids // rows_own
-    hits = iota((2 * places, tokens), 0) == owner
+def owner_slots(ids_list, half, rows_own, places, cap):
+    tokens = ids_list[0].shape[1]
+    owners = [ids // rows_own for ids in ids_list]
+    hits = [iota((2 * places, tokens), 0) == owner for owner in owners]
     earlier = (iota((tokens, tokens), 0) < iota((tokens, tokens), 1)).astype(BF16)
-    before = dot(hits.astype(BF16), earlier)
-    rank = jnp.sum(jnp.where(hits, before, 0.0), axis=0, keepdims=True).astype(I32)
-    slot = (owner % places) * cap + rank
-    return slot, (owner // places != half).astype(I32), ids - owner * rows_own
+    before = dot(jnp.concatenate([h.astype(F32) for h in hits], axis=0).astype(BF16), earlier)
+    found = []
+    for i, (ids, owner, hit) in enumerate(zip(ids_list, owners, hits)):
+        ahead = before[2 * places * i : 2 * places * (i + 1)]
+        rank = jnp.sum(jnp.where(hit, ahead, 0.0), axis=0, keepdims=True).astype(I32)
+        slot = (owner % places) * cap + rank
+        found.append((slot, (owner // places != half).astype(I32), ids - owner * rows_own))
+    return found
 
 
 def pack_body(group, places, rows_own, half_ref, token_ref, next_ref, grad_ref, out_ref, slot_ref):
@@ -66,8 +70,9 @@
 
     @pl.when(step == 0)
     def _():
-        for i, ids_ref in enumerate((token_ref, next_ref)[: 1 + group]):
-            slot, theirs, local = owner_slots(ids_ref[...], half_ref[0], rows_own, places, tokens // places)
+        ids_list = [ref[...] for ref in (token_ref, next_ref)[: 1 + group]]
+        found = owner_slots(ids_list, half_ref[0], rows_own, places, tokens // places)
+        for i, (slot, theirs, local) in enumerate(found):
             slot_ref[3 * i : 3 * i + 1] = jnp.where(theirs == group, slot, -1)
             slot_ref[3 * i + 1 : 3 * i + 2] = jnp.where(theirs == group, -1, slot)
             slot_ref[3 * i + 2 : 3 * i + 3] = local
@@ -85,7 +90,7 @@
         out_ref[:, width:] = tags.astype(BF16)
 
 
-def pack(group, places, rows_own, half, token_ids, next_ids, embed_grad, pieces=2):
+def pack(group, places, rows_own, half, token_ids, next_ids, embed_grad, pieces=1):
     tokens, width = embed_grad.shape
     total = width + LANES * group
     whole = lambda shape: pl.BlockSpec(shape, lambda i: (0, 0))
@@ -117,24 +122,34 @@
         ref[...] = chosen_rows(got_ref, lane, got_ref.shape[1] - LANES, ref.shape[1])
 
 
+def adam(param, one, two, proj, mine, other):
+    grad = proj + (mine + other)
+    one = 0.9 * one + 0.1 * grad
+    two = 0.999 * two + 0.001 * grad * grad
+    first_fix = 1.0 - 0.9**STEP
+    second_fix = 1.0 - 0.999**STEP
+    return param - 0.01 * (one / first_fix) / (jnp.sqrt(two / second_fix) + 1e-08), one, two
+
+
+def table_body(param_ref, one_ref, two_ref, proj_ref, tags_ref, got_ref, other_ref, table_ref):
+    rows, n = table_ref.shape
+    width = param_ref.shape[1]
+    mine = dot(chosen_rows(tags_ref, 2, width, rows), got_ref[:, :n], ((0,), (0,)))
+    held = (ref[:, :n] for ref in (param_ref, one_ref, two_ref, proj_ref))
+    table_ref[...] = adam(*held, mine, other_ref[:, :n])[0].astype(BF16)
+
+
 def adam_body(param_ref, one_ref, two_ref, proj_ref, tags_ref, got_ref, other_ref, p_ref, o_ref, t_ref, *table_refs):
     rows, width = param_ref.shape
     mine = dot(chosen_rows(tags_ref, 2, width, rows), got_ref[...], ((0,), (0,)))
-    grad = proj_ref[...] + (mine + other_ref[...])
-    one = 0.9 * one_ref[...] + 0.1 * grad
-    two = 0.999 * two_ref[...] + 0.001 * grad * grad
-    first_fix = 1.0 - 0.9**STEP
-    second_fix = 1.0 - 0.999**STEP
-    param = param_ref[...] - 0.01 * (one / first_fix) / (jnp.sqrt(two / second_fix) + 1e-08)
+    held = (ref[...] for ref in (param_ref, one_ref, two_ref, proj_ref))
+    param, one, two = adam(*held, mine, other_ref[...])
     o_ref[...] = one
     t_ref[...] = two
     p_ref[...] = param
     table = param.astype(BF16)
-    at = 0
-    for ref in table_refs[1:]:
-        ref[...] = table[:, at : at + ref.shape[1]]
-        at += ref.shape[1]
     table_refs[0][...] = table
+    table_refs[1][...] = table[:, width - table_refs[1].shape[1] :]
 
 
 def find_body(own_ask_ref, other_ask_ref, own_ref, other_ref, out_ref):
@@ -245,10 +260,15 @@
         flops=2 * tokens * tokens * LANES,
     )(half, next_ids.reshape(-1, 1))
     block = sds((rows_own, width), F32)
-    tables = tuple(sds((rows_own, n), BF16) for n in (width,) + CHUNKS)
-    new_param, new_one, new_two, table, *chunks = call(
-        adam_body, (block, block, block) + tables, [VMEM] * 7, flops=2 * tokens * rows_own * width,
-    )(param, moment_one, moment_two, proj_grad, tagged, got, theirs)
+    held = (param, moment_one, moment_two, proj_grad, tagged, got, theirs)
+    first = call(
+        table_body, sds((rows_own, CHUNKS[0]), BF16), [VMEM] * 7, flops=2 * tokens * rows_own * CHUNKS[0]
+    )(*held)
+    tables = tuple(sds((rows_own, n), BF16) for n in (width, CHUNKS[1]))
+    new_param, new_one, new_two, table, second = call(
+        adam_body, (block, block, block) + tables, [VMEM] * 7, flops=2 * tokens * rows_own * width
+    )(*held)
+    chunks = (first, second)
     ask_other, ask_own = call(tags_body, (sds((tokens, rows_own), BF16),) * 2, [VMEM])(tagged)
 
     def reply(own, other):
@@ -262,7 +282,9 @@
         n = replies.shape[1]
         return call(pick_body, sds((tokens, n), BF16), [VMEM] * 2, flops=4 * tokens * tokens * n)(route, replies)
 
-    others = [lax.ppermute(c, "zh", PAIR) for c in chunks]
+    others = []
+    for chunk in chunks:
+        others.append(lax.ppermute(chunk, "zh", PAIR))
     far = lax.ppermute(table, "tp", [(0, last), (last, 0)])
     far_other = lax.ppermute(table, ("zh", "tp"), [(last, ranks), (ranks, last), (ranks + last, 0), (0, ranks + last)])
     owns = [pick(reply(c, o)) for c, o in zip(chunks, others)]
@@ -280,8 +302,8 @@
     far_rows = pick(far_replies)
     out = join(me, ranks, width, None, near[0] + near[1])
     out = join(me, ranks, width, out, next_near[0])
+    out = join(me, ranks, width, out, next_near[1])
     out = join(me, ranks, width, out, [("far", 0, far_rows)])
-    out = join(me, ranks, width, out, next_near[1])
     return (new_param, new_one, new_two, out)
 
 

time: 162 us -> 168 us (1.037)
  local copies, waits for them, and re-layouts: 4 us -> 6.6 us
    unnamed x22 -> x32, local copies, waits for them, and re-layouts: 3.85 us -> 6.46 us
    ppermute x2, waiting for transfers between devices: 7.41 us -> 9.6 us  [on_device(): up2 = lax.ppermute(up, 'tp', [(i, i + 1) for i in steps[1:-1]])]
  transfers between devices with their start and end apart: 18 -> 18, of which waited for: 15 -> 14; matrix products, arithmetic and copies ran while one was open for 0% -> 0% of each run, Pallas kernels for 11% -> 10%
where the time goes in v4:
time: 168 us; the launch traced here: 166 us
  waiting for transfers between devices  68.2 us (41%)
  starting transfers between devices  63.6 us (38%)
  Pallas kernels  26.5 us (16%)
  local copies, waits for them, and re-layouts  6.6 us (4%)
    all_to_all x5, starting transfers between devices, exchange(): return lax.all_to_all(x, PLANE, split_axis=0, concat_axis=0, tiled=True)  35.6 us
    all_to_all x5, waiting for transfers between devices, exchange(): return lax.all_to_all(x, PLANE, split_axis=0, concat_axis=0, tiled=True)  24.7 us
    ppermute x2, waiting for transfers between devices, on_device(): others.append(lax.ppermute(chunk, 'zh', PAIR))  16.5 us
    ppermute x2, starting transfers between devices, on_device(): down = lax.ppermute(own, 'tp', [(i, i - 1) for i in steps[1:]])  10.5 us
    ppermute x2, waiting for transfers between devices, on_device(): up2 = lax.ppermute(up, 'tp', [(i, i + 1) for i in steps[1:-1]])  9.6 us
    pallas_call x4, Pallas kernels, join(): call(functools.partial(join_body, [p[:2] for p in pieces], ranks, width,...  9.33 us
    ppermute x2, waiting for transfers between devices, on_device(): up = lax.ppermute(own, 'tp', [(i, i + 1) for i in steps[:-1]])  8.53 us
    pallas_call x2, Pallas kernels, pack(): pl.pallas_call(functools.partial(pack_body, group, places, rows_own), gri...  6.73 us
  transfers between devices with their start and end apart: 18, of which 14 were waited for; matrix products, arithmetic and copies ran while one was open for 0% of the time, Pallas kernels for 10%

profile of v4, /device:TPU:230, one launch (start us, length us, event | category | flops | bytes accessed | tf_op | source)
XLA Modules:
  0.0 165.9 jit_solution(12008863417284083151)
XLA Ops:
  0.6 3.7 %pack.2 = bf16[512,1024]{1,0:T(8,128)(2,1)} custom-call(s32[1]{0:T(128)} %bitcast.half_ref, s32[1,512]{1,0:T(1,128)} %bitcast.26, s32[1,512]{1,0:T(1,128)} %bitcast.23, bf16[512,896]{1,0:T(8,128)(2,1)} %grad_ref.3), custom_call_target="tpu_custom_call" | custom-call | flops 469762048 | bytes 3145728 | tf_op jit(solution)/shard_map/pack/pallas_call | solution.py:97
  4.3 7.7 %all-to-all-start = ((bf16[32,16,1024]{2,1,0:T(8,128)(2,1)}), bf16[32,16,1024]{2,1,0:T(8,128)(2,1)S(1)}, u32[]{:S(2)}, u32[]{:S(2)}) async-start(bf16[32,16,1024]{2,1,0:T(8,128)(2,1)} %bitcast.21), calls=%async_computation | async-start | bytes 2097152 | tf_op jit(solution)/shard_map/all_to_all | solution.py:247
  12.0 3.1 %pack.3 = bf16[512,896]{1,0:T(8,128)(2,1)} custom-call(s32[1]{0:T(128)} %bitcast.half_ref, s32[1,512]{1,0:T(1,128)} %bitcast.27, s32[1,512]{1,0:T(1,128)} %bitcast.24, bf16[512,896]{1,0:T(8,128)(2,1)} %grad_ref.3), custom_call_target="tpu_custom_call" | custom-call | flops 469762048 | bytes 3145728 | tf_op jit(solution)/shard_map/pack/pallas_call | solution.py:97
  15.1 11.5 %all-to-all-done = bf16[32,16,1024]{2,1,0:T(8,128)(2,1)S(1)} async-done(((bf16[32,16,1024]{2,1,0:T(8,128)(2,1)}), bf16[32,16,1024]{2,1,0:T(8,128)(2,1)S(1)}, u32[]{:S(2)}, u32[]{:S(2)}) %all-to-all-start) | async-done | bytes 1048608 | tf_op jit(solution)/shard_map/all_to_all | solution.py:247
  26.6 6.4 %all-to-all-start.1 = ((bf16[32,16,896]{2,1,0:T(8,128)(2,1)}), bf16[32,16,896]{2,1,0:T(8,128)(2,1)S(1)}, u32[]{:S(2)}, u32[]{:S(2)}) async-start(bf16[32,16,896]{2,1,0:T(8,128)(2,1)} %bitcast.22), calls=%async_computation.1 | async-start | bytes 1835008 | tf_op jit(solution)/shard_map/all_to_all | solution.py:247
  33.5 1.5 collective-permute-start
  35.0 11.4 %all-to-all-done.1 = bf16[32,16,896]{2,1,0:T(8,128)(2,1)S(1)} async-done(((bf16[32,16,896]{2,1,0:T(8,128)(2,1)}), bf16[32,16,896]{2,1,0:T(8,128)(2,1)S(1)}, u32[]{:S(2)}, u32[]{:S(2)}) %all-to-all-start.1) | async-done | bytes 917536 | tf_op jit(solution)/shard_map/all_to_all | solution.py:247
  46.5 1.7 %collective-permute-done.other_ref = f32[64,896]{1,0:T(8,128)S(1)} collective-permute-done((f32[64,896]{1,0:T(8,128)S(1)}, f32[64,896]{1,0:T(8,128)S(1)}, u32[]{:S(2)}, u32[]{:S(2)}) %collective-permute-start) | collective-permute-done | bytes 229408 | tf_op jit(solution)/shard_map/ppermute | solution.py:256
  50.8 7.4 %collective-permute-done.4.other_ref = bf16[64,384]{1,0:T(8,128)(2,1)S(1)} collective-permute-done((bf16[64,384]{1,0:T(8,128)(2,1)S(1)}, bf16[64,384]{1,0:T(8,128)(2,1)S(1)}, u32[]{:S(2)}, u32[]{:S(2)}) %collective-permute-start.4) | collective-permute-done | bytes 49184 | tf_op jit(solution)/shard_map/ppermute | solution.py:287
  59.4 7.5 %all-to-all-start.3 = ((bf16[32,32,384]{2,1,0:T(8,128)(2,1)}), bf16[32,32,384]{2,1,0:T(8,128)(2,1)S(1)}, u32[]{:S(2)}, u32[]{:S(2)}) async-start(bf16[32,32,384]{2,1,0:T(8,128)(2,1)} %shard_map.109), calls=%async_computation.3 | async-start | bytes 1572864 | tf_op jit(solution)/shard_map/all_to_all | solution.py:247
  70.6 9.2 %collective-permute-done.1.other_ref = bf16[64,512]{1,0:T(8,128)(2,1)S(1)} collective-permute-done((bf16[64,512]{1,0:T(8,128)(2,1)S(1)}, bf16[64,512]{1,0:T(8,128)(2,1)S(1)}, u32[]{:S(2)}, u32[]{:S(2)}) %collective-permute-start.1) | collective-permute-done | bytes 65568 | tf_op jit(solution)/shard_map/ppermute | solution.py:287
  81.2 7.5 %all-to-all-start.2 = ((bf16[32,32,512]{2,1,0:T(8,128)(2,1)}), bf16[32,32,512]{2,1,0:T(8,128)(2,1)S(1)}, u32[]{:S(2)}, u32[]{:S(2)}) async-start(bf16[32,32,512]{2,1,0:T(8,128)(2,1)} %shard_map.107), calls=%async_computation.2 | async-start | bytes 2097152 | tf_op jit(solution)/shard_map/all_to_all | solution.py:247
  88.7 1.9 %collective-permute-start.12 = (bf16[64,896]{1,0:T(8,128)(2,1)}, bf16[64,896]{1,0:T(8,128)(2,1)S(1)}, u32[]{:S(2)}, u32[]{:S(2)}) collective-permute-start(bf16[64,896]{1,0:T(8,128)(2,1)} %copy-done.14), channel_id=1, source_target_pairs={{3,128},{128,3},{131,0},{0,131},{7,132},{132,7},{135,4},{4,135},{1... | collective-permute-start | bytes 344072 | tf_op jit(solution)/shard_map/ppermute | solution.py:289
  90.6 5.1 %collective-permute-start.11 = (bf16[64,896]{1,0:T(8,128)(2,1)}, bf16[64,896]{1,0:T(8,128)(2,1)S(1)}, u32[]{:S(2)}, u32[]{:S(2)}) collective-permute-start(bf16[64,896]{1,0:T(8,128)(2,1)} %copy-done.14), channel_id=1, source_target_pairs={{0,3},{3,0},{4,7},{7,4},{8,11},{11,8},{12,15},{15,12},{16,19},{19,... | collective-permute-start | bytes 344072 | tf_op jit(solution)/shard_map/ppermute | solution.py:288
  95.8 1.4 collective-permute-done.12.other_ref
  97.2 2.5 %collective-permute-done.11.own_ref = bf16[64,896]{1,0:T(8,128)(2,1)S(1)} collective-permute-done((bf16[64,896]{1,0:T(8,128)(2,1)}, bf16[64,896]{1,0:T(8,128)(2,1)S(1)}, u32[]{:S(2)}, u32[]{:S(2)}) %collective-permute-start.11) | collective-permute-done | bytes 114720 | tf_op jit(solution)/shard_map/ppermute | solution.py:288
  99.7 1.9 %shard_map.114 = bf16[32,32,896]{2,1,0:T(8,128)(2,1)} custom-call(bf16[512,64]{1,0:T(8,128)(2,1)S(1)} %get-tuple-element.14.own_ask_ref, bf16[512,64]{1,0:T(8,128)(2,1)S(1)} %get-tuple-element.15.other_ask_ref, bf16[64,896]{1,0:T(8,128)(2,1)S(1)} %collective-permute-done.11.own_ref, bf16[64,896]{1,0:T(8,128)(2,1)S(1)} %collective-permute-done.12.other_ref), custom_call_target="tpu_custom_call" | custom-call | flops 117440512 | bytes 1048576 | tf_op jit(solution)/shard_map/pallas_call | solution.py:276
  101.6 1.7 %all-to-all-done.2 = bf16[32,32,512]{2,1,0:T(8,128)(2,1)S(1)} async-done(((bf16[32,32,512]{2,1,0:T(8,128)(2,1)}), bf16[32,32,512]{2,1,0:T(8,128)(2,1)S(1)}, u32[]{:S(2)}, u32[]{:S(2)}) %all-to-all-start.2) | async-done | bytes 1048608 | tf_op jit(solution)/shard_map/all_to_all | solution.py:247
  103.3 6.5 %all-to-all-start.4 = ((bf16[32,32,896]{2,1,0:T(8,128)(2,1)}), bf16[32,32,896]{2,1,0:T(8,128)(2,1)S(1)}, u32[]{:S(2)}, u32[]{:S(2)}) async-start(bf16[32,32,896]{2,1,0:T(8,128)(2,1)} %shard_map.114), calls=%async_computation.4 | async-start | bytes 3670016 | tf_op jit(solution)/shard_map/all_to_all | solution.py:247
  113.0 5.2 %collective-permute-start.3 = (bf16[512,512]{1,0:T(8,128)(2,1)S(1)}, bf16[512,512]{1,0:T(8,128)(2,1)}, u32[]{:S(2)}, u32[]{:S(2)}) collective-permute-start(bf16[512,512]{1,0:T(8,128)(2,1)S(1)} %shard_map.108.refs_0_), channel_id=1, source_target_pairs={{1,0},{2,1},{3,2},{5,4},{6,5},{7,6},{9,8},{10,9},{11,10},{13,12},{... | collective-permute-start | bytes 1572872 | tf_op jit(solution)/shard_map/ppermute | solution.py:296
  120.1 5.3 %collective-permute-start.6 = (bf16[512,384]{1,0:T(8,128)(2,1)S(1)}, bf16[512,384]{1,0:T(8,128)(2,1)}, u32[]{:S(2)}, u32[]{:S(2)}) collective-permute-start(bf16[512,384]{1,0:T(8,128)(2,1)S(1)} %shard_map.110.refs_3_), channel_id=1, source_target_pairs={{1,0},{2,1},{3,2},{5,4},{6,5},{7,6},{9,8},{10,9},{11,10},{13,12},{... | collective-permute-start | bytes 1179656 | tf_op jit(solution)/shard_map/ppermute | solution.py:296
  127.5 2.2 %collective-permute-done.3.refs_2_ = bf16[512,512]{1,0:T(8,128)(2,1)} collective-permute-done((bf16[512,512]{1,0:T(8,128)(2,1)S(1)}, bf16[512,512]{1,0:T(8,128)(2,1)}, u32[]{:S(2)}, u32[]{:S(2)}) %collective-permute-start.3) | collective-permute-done | bytes 524320 | tf_op jit(solution)/shard_map/ppermute | solution.py:296
  129.6 1.5 collective-permute-start.8
  131.1 3.8 %collective-permute-done.2.refs_1_ = bf16[512,512]{1,0:T(8,128)(2,1)} collective-permute-done((bf16[512,512]{1,0:T(8,128)(2,1)S(1)}, bf16[512,512]{1,0:T(8,128)(2,1)}, u32[]{:S(2)}, u32[]{:S(2)}) %collective-permute-start.2) | collective-permute-done | bytes 524320 | tf_op jit(solution)/shard_map/ppermute | solution.py:295
  137.2 1.4 collective-permute-start.10
  138.6 4.7 %collective-permute-done.5.refs_4_ = bf16[512,384]{1,0:T(8,128)(2,1)} collective-permute-done((bf16[512,384]{1,0:T(8,128)(2,1)S(1)}, bf16[512,384]{1,0:T(8,128)(2,1)}, u32[]{:S(2)}, u32[]{:S(2)}) %collective-permute-start.5) | collective-permute-done | bytes 393248 | tf_op jit(solution)/shard_map/ppermute | solution.py:295
  145.6 3.5 %shard_map.111.refs_0_ = bf16[512,3584]{1,0:T(8,128)(2,1)} custom-call(s32[1]{0:T(128)} %bitcast.7.me_ref, bf16[512,512]{1,0:T(8,128)(2,1)S(1)} %shard_map.108.refs_0_, bf16[512,512]{1,0:T(8,128)(2,1)} %collective-permute-done.2.refs_1_, bf16[512,512]{1,0:T(8,128)(2,1)} %collective-permute-done.3.refs_2_, bf16[512,384]{1,0:T(8,128)(2,1)S(1)} %copy-done.5, ...), custom_call_target="tpu_custom_call" | custom-call | bytes 2097152 | tf_op jit(solution)/shard_map/pallas_call | solution.py:224
  150.4 4.2 %collective-permute-done.7.refs_1_ = bf16[512,512]{1,0:T(8,128)(2,1)} collective-permute-done((bf16[512,512]{1,0:T(8,128)(2,1)}, bf16[512,512]{1,0:T(8,128)(2,1)}, u32[]{:S(2)}, u32[]{:S(2)}) %collective-permute-start.7) | collective-permute-done | bytes 524320 | tf_op jit(solution)/shard_map/ppermute | solution.py:297
  154.6 1.9 %shard_map.112.refs_0_ = bf16[512,3584]{1,0:T(8,128)(2,1)} custom-call(s32[1]{0:T(128)} %bitcast.7.me_ref, bf16[512,3584]{1,0:T(8,128)(2,1)} %shard_map.111.refs_0_, bf16[512,512]{1,0:T(8,128)(2,1)} %collective-permute-done.7.refs_1_, bf16[512,512]{1,0:T(8,128)(2,1)} %collective-permute-done.8.refs_2_), custom_call_target="tpu_custom_call", output_to_operand_aliasing={{}: (1, {})} | custom-call | bytes 2097152 | tf_op jit(solution)/shard_map/pallas_call | solution.py:224
  156.5 5.4 %collective-permute-done.9.refs_1_ = bf16[512,384]{1,0:T(8,128)(2,1)} collective-permute-done((bf16[512,384]{1,0:T(8,128)(2,1)}, bf16[512,384]{1,0:T(8,128)(2,1)}, u32[]{:S(2)}, u32[]{:S(2)}) %collective-permute-start.9) | collective-permute-done | bytes 393248 | tf_op jit(solution)/shard_map/ppermute | solution.py:297
  161.9 1.8 %shard_map.113.refs_0_ = bf16[512,3584]{1,0:T(8,128)(2,1)} custom-call(s32[1]{0:T(128)} %bitcast.7.me_ref, bf16[512,3584]{1,0:T(8,128)(2,1)} %shard_map.112.refs_0_, bf16[512,384]{1,0:T(8,128)(2,1)} %collective-permute-done.9.refs_1_, bf16[512,384]{1,0:T(8,128)(2,1)} %collective-permute-done.10.refs_2_), custom_call_target="tpu_custom_call", output_to_operand_aliasing={{}: (1, {})} | custom-call | bytes 2097152 | tf_op jit(solution)/shard_map/pallas_call | solution.py:224
  163.7 2.2 %shard_map.116 = bf16[512,3584]{1,0:T(8,128)(2,1)} custom-call(s32[1]{0:T(128)} %bitcast.7.me_ref, bf16[512,3584]{1,0:T(8,128)(2,1)} %shard_map.113.refs_0_, bf16[512,896]{1,0:T(8,128)(2,1)S(1)} %shard_map.115.refs_1_), custom_call_target="tpu_custom_call", output_to_operand_aliasing={{}: (1, {})} | custom-call | bytes 2097152 | tf_op jit(solution)/shard_map/pallas_call | solution.py:224
  (54 shorter events, 22.3 us)
Async XLA Ops:
  4.3 43.9 %copy-start.6 = (f32[64,896]{1,0:T(8,128)S(1)}, f32[64,896]{1,0:T(8,128)}, u32[]{:S(2)}) copy-start(f32[64,896]{1,0:T(8,128)} %param_ref.3) | copy-start | bytes 688132
  4.3 43.9 %copy-start.7 = (f32[64,896]{1,0:T(8,128)S(1)}, f32[64,896]{1,0:T(8,128)}, u32[]{:S(2)}) copy-start(f32[64,896]{1,0:T(8,128)} %one_ref.3) | copy-start | bytes 688132
  4.3 43.9 %copy-start.8 = (f32[64,896]{1,0:T(8,128)S(1)}, f32[64,896]{1,0:T(8,128)}, u32[]{:S(2)}) copy-start(f32[64,896]{1,0:T(8,128)} %two_ref.3) | copy-start | bytes 688132
  4.3 43.9 %copy-start.10 = (f32[64,896]{1,0:T(8,128)S(1)}, f32[64,896]{1,0:T(8,128)}, u32[]{:S(2)}) copy-start(f32[64,896]{1,0:T(8,128)} %proj_ref.3) | copy-start | bytes 688132
  4.3 22.3 %all-to-all-start = ((bf16[32,16,1024]{2,1,0:T(8,128)(2,1)}), bf16[32,16,1024]{2,1,0:T(8,128)(2,1)S(1)}, u32[]{:S(2)}, u32[]{:S(2)}) async-start(bf16[32,16,1024]{2,1,0:T(8,128)(2,1)} %bitcast.21), calls=%async_computation | async-start | bytes 2097152 | tf_op jit(solution)/shard_map/all_to_all | solution.py:247
  26.6 19.8 %all-to-all-start.1 = ((bf16[32,16,896]{2,1,0:T(8,128)(2,1)}), bf16[32,16,896]{2,1,0:T(8,128)(2,1)S(1)}, u32[]{:S(2)}, u32[]{:S(2)}) async-start(bf16[32,16,896]{2,1,0:T(8,128)(2,1)} %bitcast.22), calls=%async_computation.1 | async-start | bytes 1835008 | tf_op jit(solution)/shard_map/all_to_all | solution.py:247
  33.5 14.7 %collective-permute-start = (f32[64,896]{1,0:T(8,128)S(1)}, f32[64,896]{1,0:T(8,128)S(1)}, u32[]{:S(2)}, u32[]{:S(2)}) collective-permute-start(f32[64,896]{1,0:T(8,128)S(1)} %shard_map.102), channel_id=1, source_target_pairs={{0,128},{128,0},{1,129},{129,1},{2,130},{130,2},{3,131},{131,3},{4... | collective-permute-start | bytes 688136 | tf_op jit(solution)/shard_map/ppermute | solution.py:256
  48.2 11.3 %copy-start.12 = (f32[64,896]{1,0:T(8,128)}, f32[64,896]{1,0:T(8,128)S(1)}, u32[]{:S(2)}) copy-start(f32[64,896]{1,0:T(8,128)S(1)} %collective-permute-done.other_ref) | copy-start | bytes 688132
  50.2 8.0 %collective-permute-start.4 = (bf16[64,384]{1,0:T(8,128)(2,1)S(1)}, bf16[64,384]{1,0:T(8,128)(2,1)S(1)}, u32[]{:S(2)}, u32[]{:S(2)}) collective-permute-start(bf16[64,384]{1,0:T(8,128)(2,1)S(1)} %get-tuple-element.16.own_ref), channel_id=1, source_target_pairs={{0,128},{128,0},{1,129},{129,1},{2,130},{130,2},{3,131},{131,3},{4... | collective-permute-start | bytes 147464 | tf_op jit(solution)/shard_map/ppermute | solution.py:287
  59.4 21.8 %all-to-all-start.3 = ((bf16[32,32,384]{2,1,0:T(8,128)(2,1)}), bf16[32,32,384]{2,1,0:T(8,128)(2,1)S(1)}, u32[]{:S(2)}, u32[]{:S(2)}) async-start(bf16[32,32,384]{2,1,0:T(8,128)(2,1)} %shard_map.109), calls=%async_computation.3 | async-start | bytes 1572864 | tf_op jit(solution)/shard_map/all_to_all | solution.py:247
  66.9 0.9 copy-start.9
  67.8 0.9 copy-start.11
  68.8 0.9 copy-start.13
  70.1 9.7 %collective-permute-start.1 = (bf16[64,512]{1,0:T(8,128)(2,1)S(1)}, bf16[64,512]{1,0:T(8,128)(2,1)S(1)}, u32[]{:S(2)}, u32[]{:S(2)}) collective-permute-start(bf16[64,512]{1,0:T(8,128)(2,1)S(1)} %shard_map.106.own_ref), channel_id=1, source_target_pairs={{0,128},{128,0},{1,129},{129,1},{2,130},{130,2},{3,131},{131,3},{4... | collective-permute-start | bytes 196616 | tf_op jit(solution)/shard_map/ppermute | solution.py:287
  81.2 28.7 %copy-start.15 = (s32[512]{0:T(512)S(1)}, s32[512]{0:T(512)}, u32[]{:S(2)}) copy-start(s32[512]{0:T(512)} %param.13) | copy-start | bytes 6148
  81.2 22.1 %copy-start.2 = (bf16[32,32,384]{2,1,0:T(8,128)(2,1)}, bf16[32,32,384]{2,1,0:T(8,128)(2,1)S(1)}, u32[]{:S(2)}) copy-start(bf16[32,32,384]{2,1,0:T(8,128)(2,1)S(1)} %all-to-all-done.3) | copy-start | bytes 2359300
  81.2 22.1 %all-to-all-start.2 = ((bf16[32,32,512]{2,1,0:T(8,128)(2,1)}), bf16[32,32,512]{2,1,0:T(8,128)(2,1)S(1)}, u32[]{:S(2)}, u32[]{:S(2)}) async-start(bf16[32,32,512]{2,1,0:T(8,128)(2,1)} %shard_map.107), calls=%async_computation.2 | async-start | bytes 2097152 | tf_op jit(solution)/shard_map/all_to_all | solution.py:247
  88.7 8.5 %collective-permute-start.12 = (bf16[64,896]{1,0:T(8,128)(2,1)}, bf16[64,896]{1,0:T(8,128)(2,1)S(1)}, u32[]{:S(2)}, u32[]{:S(2)}) collective-permute-start(bf16[64,896]{1,0:T(8,128)(2,1)} %copy-done.14), channel_id=1, source_target_pairs={{3,128},{128,3},{131,0},{0,131},{7,132},{132,7},{135,4},{4,135},{1... | collective-permute-start | bytes 344072 | tf_op jit(solution)/shard_map/ppermute | solution.py:289
  90.6 9.1 %collective-permute-start.11 = (bf16[64,896]{1,0:T(8,128)(2,1)}, bf16[64,896]{1,0:T(8,128)(2,1)S(1)}, u32[]{:S(2)}, u32[]{:S(2)}) collective-permute-start(bf16[64,896]{1,0:T(8,128)(2,1)} %copy-done.14), channel_id=1, source_target_pairs={{0,3},{3,0},{4,7},{7,4},{8,11},{11,8},{12,15},{15,12},{16,19},{19,... | collective-permute-start | bytes 344072 | tf_op jit(solution)/shard_map/ppermute | solution.py:288
  103.3 6.5 %copy-start = (bf16[32,32,512]{2,1,0:T(8,128)(2,1)}, bf16[32,32,512]{2,1,0:T(8,128)(2,1)S(1)}, u32[]{:S(2)}) copy-start(bf16[32,32,512]{2,1,0:T(8,128)(2,1)S(1)} %all-to-all-done.2) | copy-start | bytes 3145732
  103.3 45.8 %all-to-all-start.4 = ((bf16[32,32,896]{2,1,0:T(8,128)(2,1)}), bf16[32,32,896]{2,1,0:T(8,128)(2,1)S(1)}, u32[]{:S(2)}, u32[]{:S(2)}) async-start(bf16[32,32,896]{2,1,0:T(8,128)(2,1)} %shard_map.114), calls=%async_computation.4 | async-start | bytes 3670016 | tf_op jit(solution)/shard_map/all_to_all | solution.py:247
  110.0 9.4 %copy-start.3 = (bf16[32,32,384]{2,1,0:T(8,128)(2,1)S(1)}, bf16[32,32,384]{2,1,0:T(8,128)(2,1)}, u32[]{:S(2)}) copy-start(bf16[32,32,384]{2,1,0:T(8,128)(2,1)} %copy-done.2) | copy-start | bytes 2359300
  111.0 1.2 copy-start.1
  113.0 16.7 %collective-permute-start.3 = (bf16[512,512]{1,0:T(8,128)(2,1)S(1)}, bf16[512,512]{1,0:T(8,128)(2,1)}, u32[]{:S(2)}, u32[]{:S(2)}) collective-permute-start(bf16[512,512]{1,0:T(8,128)(2,1)S(1)} %shard_map.108.refs_0_), channel_id=1, source_target_pairs={{1,0},{2,1},{3,2},{5,4},{6,5},{7,6},{9,8},{10,9},{11,10},{13,12},{... | collective-permute-start | bytes 1572872 | tf_op jit(solution)/shard_map/ppermute | solution.py:296
  118.1 16.8 %collective-permute-start.2 = (bf16[512,512]{1,0:T(8,128)(2,1)S(1)}, bf16[512,512]{1,0:T(8,128)(2,1)}, u32[]{:S(2)}, u32[]{:S(2)}) collective-permute-start(bf16[512,512]{1,0:T(8,128)(2,1)S(1)} %shard_map.108.refs_0_), channel_id=1, source_target_pairs={{0,1},{1,2},{2,3},{4,5},{5,6},{6,7},{8,9},{9,10},{10,11},{12,13},{... | collective-permute-start | bytes 1572872 | tf_op jit(solution)/shard_map/ppermute | solution.py:295
  120.1 17.1 %collective-permute-start.6 = (bf16[512,384]{1,0:T(8,128)(2,1)S(1)}, bf16[512,384]{1,0:T(8,128)(2,1)}, u32[]{:S(2)}, u32[]{:S(2)}) collective-permute-start(bf16[512,384]{1,0:T(8,128)(2,1)S(1)} %shard_map.110.refs_3_), channel_id=1, source_target_pairs={{1,0},{2,1},{3,2},{5,4},{6,5},{7,6},{9,8},{10,9},{11,10},{13,12},{... | collective-permute-start | bytes 1179656 | tf_op jit(solution)/shard_map/ppermute | solution.py:296
  125.5 17.9 %collective-permute-start.5 = (bf16[512,384]{1,0:T(8,128)(2,1)S(1)}, bf16[512,384]{1,0:T(8,128)(2,1)}, u32[]{:S(2)}, u32[]{:S(2)}) collective-permute-start(bf16[512,384]{1,0:T(8,128)(2,1)S(1)} %shard_map.110.refs_3_), channel_id=1, source_target_pairs={{0,1},{1,2},{2,3},{4,5},{5,6},{6,7},{8,9},{9,10},{10,11},{12,13},{... | collective-permute-start | bytes 1179656 | tf_op jit(solution)/shard_map/ppermute | solution.py:295
  129.6 20.7 %collective-permute-start.8 = (bf16[512,512]{1,0:T(8,128)(2,1)}, bf16[512,512]{1,0:T(8,128)(2,1)}, u32[]{:S(2)}, u32[]{:S(2)}) collective-permute-start(bf16[512,512]{1,0:T(8,128)(2,1)} %collective-permute-done.3.refs_2_), channel_id=1, source_target_pairs={{1,0},{2,1},{5,4},{6,5},{9,8},{10,9},{13,12},{14,13},{17,16},{18,1... | collective-permute-start | bytes 1572872 | tf_op jit(solution)/shard_map/ppermute | solution.py:298
  134.9 19.7 %collective-permute-start.7 = (bf16[512,512]{1,0:T(8,128)(2,1)}, bf16[512,512]{1,0:T(8,128)(2,1)}, u32[]{:S(2)}, u32[]{:S(2)}) collective-permute-start(bf16[512,512]{1,0:T(8,128)(2,1)} %collective-permute-done.2.refs_1_), channel_id=1, source_target_pairs={{1,2},{2,3},{5,6},{6,7},{9,10},{10,11},{13,14},{14,15},{17,18},{18... | collective-permute-start | bytes 1572872 | tf_op jit(solution)/shard_map/ppermute | solution.py:297
  137.2 19.3 %collective-permute-start.10 = (bf16[512,384]{1,0:T(8,128)(2,1)}, bf16[512,384]{1,0:T(8,128)(2,1)}, u32[]{:S(2)}, u32[]{:S(2)}) collective-permute-start(bf16[512,384]{1,0:T(8,128)(2,1)} %collective-permute-done.6.refs_5_), channel_id=1, source_target_pairs={{1,0},{2,1},{5,4},{6,5},{9,8},{10,9},{13,12},{14,13},{17,16},{18,1... | collective-permute-start | bytes 1179656 | tf_op jit(solution)/shard_map/ppermute | solution.py:298
  143.3 18.5 %collective-permute-start.9 = (bf16[512,384]{1,0:T(8,128)(2,1)}, bf16[512,384]{1,0:T(8,128)(2,1)}, u32[]{:S(2)}, u32[]{:S(2)}) collective-permute-start(bf16[512,384]{1,0:T(8,128)(2,1)} %collective-permute-done.5.refs_4_), channel_id=1, source_target_pairs={{1,2},{2,3},{5,6},{6,7},{9,10},{10,11},{13,14},{14,15},{17,18},{18... | collective-permute-start | bytes 1179656 | tf_op jit(solution)/shard_map/ppermute | solution.py:297
  144.6 1.0 copy-start.5
  (2 other events, 1.4 us)
